TPU v7x, 128 devices: a whole 4x4x4 slice. The times are simulated.
128 devices in a mesh: task: 8 (over y, z_hi), width: 16 (over z_lo, x, core).
Axes of the slice: x: 4, y: 4, z: 4 (z_hi: 2, z_lo: 2; z = z_hi * 2 + z_lo), core: 2. Of those that a mesh axis runs over, the one named last changes fastest.
Arguments:
- task_ids: int32 [1024], P('task'), may hold values from 0 to 1023
- embed_table: bfloat16 [1024, 1024], replicated, may hold values from -6 to 6
- trunk_weight: bfloat16 [1024, 2048], replicated, may hold values from -0.1875 to 0.1875
- trunk_bias: float32 [2048], replicated, may hold values from -6 to 6
- head_weight: bfloat16 [2048, 262144], P(None, ('task', 'width')), may hold values from -0.125 to 0.125
- head_bias: float32 [262144], P(('task', 'width')), may hold values from -4 to 4
- token_row: int32 [32768], P('task'), may hold values from 0 to 1023, as said below
- inputs: bfloat16 [32768, 8192], P('task', 'width'), may hold values from -6 to 6
- frozen: bfloat16 [32768, 8192], P('task', 'width'), may hold values from -6 to 6
Outputs:
- adapted: bfloat16 [32768, 8192], P('task', 'width')
Inputs may be any that keep to these rules, and one draw needn't show every extreme that they name: `token_row`: each of the 1024 rows is named by exactly 32 tokens, and tokens b * 4096 to (b + 1) * 4096 - 1 name only rows b * 128 to (b + 1) * 128 - 1.
All inputs are finite; a program needn't handle non-finite values.
Results may differ from a plain program's by a relative error of at most 0.0061.
Values may be sent and summed in bfloat16 or wider, within the bound.
No kernel may reach another device: no remote copies, remote signals or barrier semaphores. Data moves between devices by JAX's collectives and lax.ppermute only.
A program may use at most 128 MiB of HBM per device.

v0:
```python
import math

import jax
import jax.numpy as jnp
from jax import lax
from jax.sharding import PartitionSpec as P

WIDTH = 8192
RANK = 16


def laid_out(tiles, dim):
    tiles = jnp.moveaxis(tiles, 0, dim)
    lengths = tiles.shape
    return tiles.reshape(*lengths[:dim], lengths[dim] * lengths[dim + 1], *lengths[dim + 2 :])


def sent_to_all(shard, axis):
    length = lax.axis_size(axis)
    return lax.all_to_all(
        jnp.broadcast_to(shard[None], (length, *shard.shape)), axis, 0, 0, tiled=True
    )


def collect(shard, axis, dim):
    return laid_out(sent_to_all(shard, axis), dim)


def total_of_pieces(shard, axis):
    tiles = lax.all_gather(shard, axis)
    return tiles.sum(axis=0)


def run_trunk(id_values, embed_table, trunk_weight, trunk_bias):
    one_hot = (
        id_values[:, None] == jnp.arange(embed_table.shape[0], dtype=jnp.int32)[None, :]
    ).astype(jnp.bfloat16)
    embedded = jnp.dot(one_hot, embed_table, preferred_element_type=jnp.float32).astype(
        jnp.bfloat16
    )
    preact = jnp.dot(embedded, trunk_weight, preferred_element_type=jnp.float32) + trunk_bias
    return jax.nn.silu(preact).astype(jnp.bfloat16)


def on_device(
    task_ids,
    embed_table,
    trunk_weight,
    trunk_bias,
    head_weight,
    head_bias,
    token_row,
    inputs,
    frozen,
):
    task_count = lax.axis_size("task")
    width_count = lax.axis_size("width")
    rows_dev = task_ids.shape[0]
    all_ids = collect(task_ids, "task", 0)
    hidden = run_trunk(all_ids, embed_table, trunk_weight, trunk_bias)
    inner_cols = head_weight.shape[1] // width_count
    weight_cube = head_weight.reshape(head_weight.shape[0], inner_cols, width_count)
    hidden_rows = hidden.reshape(task_count, rows_dev, hidden.shape[1])
    head_out = jnp.einsum(
        "tqh,hks->qtsk", hidden_rows, weight_cube, preferred_element_type=jnp.float32
    )
    bias_grid = head_bias.reshape(inner_cols, width_count).T
    factors = (head_out + bias_grid[None, None, :, :]).astype(jnp.bfloat16)
    moved = lax.all_to_all(
        factors.reshape(rows_dev, task_count * width_count, inner_cols),
        ("task", "width"),
        split_axis=1,
        concat_axis=1,
        tiled=True,
    )
    slice_width = inputs.shape[1]
    grouped = moved.reshape(rows_dev, 2, RANK, slice_width)
    entry_flat = grouped[:, 0].reshape(rows_dev * RANK, slice_width)
    exit_flat = grouped[:, 1].reshape(rows_dev * RANK, slice_width)
    tok_count = inputs.shape[0]
    block_len = math.gcd(tok_count, 512)
    block_count = tok_count // block_len
    local_row = token_row - lax.axis_index("task") * rows_dev
    row_ids = jnp.arange(rows_dev, dtype=jnp.int32)
    input_blocks = inputs.reshape(block_count, block_len, slice_width)
    frozen_blocks = frozen.reshape(block_count, block_len, slice_width)
    row_blocks = local_row.reshape(block_count, block_len)

    def rank_block(block_data):
        tokens_in, rows_in = block_data
        selector = (rows_in[:, None] == row_ids[None, :]).astype(jnp.float32)
        scores = jnp.einsum("te,ke->tk", tokens_in, entry_flat, preferred_element_type=jnp.float32)
        return jnp.sum(scores.reshape(block_len, rows_dev, RANK) * selector[:, :, None], axis=1)

    rank_part = lax.map(rank_block, (input_blocks, row_blocks))
    rank_sum = total_of_pieces(rank_part, "width")
    rank_coef = (rank_sum * (1.0 / math.sqrt(WIDTH))).astype(jnp.bfloat16)

    def update_block(block_data):
        coef_in, frozen_in, rows_in = block_data
        selector = (rows_in[:, None] == row_ids[None, :]).astype(jnp.bfloat16)
        spread = (selector[:, :, None] * coef_in[:, None, :]).reshape(block_len, rows_dev * RANK)
        update = jnp.dot(spread, exit_flat, preferred_element_type=jnp.float32)
        return (frozen_in.astype(jnp.float32) + update * (1.0 / math.sqrt(RANK))).astype(
            jnp.bfloat16
        )

    result = lax.map(update_block, (rank_coef, frozen_blocks, row_blocks))
    return result.reshape(tok_count, slice_width)


def solution(mesh):
    return jax.shard_map(
        on_device,
        mesh=mesh,
        in_specs=(
            P("task"),
            P(),
            P(),
            P(),
            P(None, ("task", "width")),
            P(("task", "width")),
            P("task"),
            P("task", "width"),
            P("task", "width"),
        ),
        out_specs=P("task", "width"),
        check_vma=False,
    )
```

profile of v0, /device:TPU:1, one launch (start us, length us, event | category | flops | bytes accessed | tf_op | source)
XLA Modules:
  0.0 264.4 jit_solution(3720756659738714810)
XLA Ops:
  6.5 1.4 broadcast_in_dim.18
  7.9 8.3 %all-to-all-start = ((s32[8,1,128]{2,1,0:T(1,128)}), s32[8,1,128]{2,1,0:T(1,128)S(1)}, u32[]{:S(2)}, u32[]{:S(2)}) async-start(s32[8,1,128]{2,1,0:T(1,128)} %broadcast_in_dim.18), calls=%async_computation | async-start | bytes 8192 | tf_op jit(solution)/shard_map/all_to_all | solution.py:20
  16.3 12.4 %copy.25 = bf16[2048,2048]{0,1:T(8,128)(2,1)} copy(bf16[2048,2048]{1,0:T(8,128)(2,1)} %param.17) | data formatting | bytes 16777216 | tf_op args[4]
  28.6 12.5 %copy.26 = bf16[2048,128,16]{1,0,2:T(8,128)(2,1)} copy(bf16[2048,128,16]{0,2,1:T(8,128)(2,1)} %bitcast.72) | data formatting | bytes 16777216 | tf_op jit(solution)/shard_map/reshape | solution.py:62
  41.3 11.5 %multiply_convert_fusion = bf16[1024,2048]{1,0:T(8,128)(2,1)} fusion(f32[2048]{0:T(1024)S(1)} %copy-done.4, bf16[1024,2048]{1,0:T(8,128)(2,1)} %param.15, bf16[1024,1024]{1,0:T(8,128)(2,1)S(1)} %copy-done, s32[1024]{0:T(1024)S(1)} %bitcast.81), kind=kOutput, calls=%fused_computation.25 | convolution fusion | flops 6457131008 | bytes 10498048 | tf_op jit(solution)/shard_map/dot_general | solution.py:41
  52.8 13.8 %fusion.14 = bf16[128,8,16,128]{3,0,2,1:T(8,128)(2,1)} fusion(f32[16,128]{1,0:T(8,128)S(1)} %copy.27, bf16[8,128,2048,1]{2,1,3,0:T(8,128)(2,1)} %bitcast.84, bf16[2048,128,16]{1,0,2:T(8,128)(2,1)} %copy.26), kind=kOutput, calls=%fused_computation.22 | convolution fusion | flops 8594128896 | bytes 16785408 | tf_op jit(solution)/shard_map/tqh,hks->qtsk/dot_general | solution.py:64
  66.6 6.4 %copy.28 = bf16[128,128,128]{0,2,1:T(8,128)(2,1)} copy(bf16[128,128,128]{2,0,1:T(8,128)(2,1)} %bitcast.74) | data formatting | bytes 8388608 | tf_op jit(solution)/shard_map/reshape | solution.py:70
  73.0 10.8 %all-to-all-start.1 = ((bf16[128,128,128]{0,2,1:T(8,128)(2,1)}), bf16[128,128,128]{0,2,1:T(8,128)(2,1)}, u32[]{:S(2)}, u32[]{:S(2)}) async-start(bf16[128,128,128]{0,2,1:T(8,128)(2,1)} %copy.28), calls=%async_computation.1 | async-start | bytes 8388608 | tf_op jit(solution)/shard_map/all_to_all | solution.py:69
  83.8 0.2 all-gather.3.cloned.1.call-start
  84.1 52.3 %all-to-all-done.1 = bf16[128,128,128]{0,2,1:T(8,128)(2,1)} async-done(((bf16[128,128,128]{0,2,1:T(8,128)(2,1)}), bf16[128,128,128]{0,2,1:T(8,128)(2,1)}, u32[]{:S(2)}, u32[]{:S(2)}) %all-to-all-start.1) | async-done | bytes 4194336 | tf_op jit(solution)/shard_map/all_to_all | solution.py:69
  136.4 4.0 %fusion.22 = (bf16[128,1,16,512]{0,3,2,1:T(8,128)(2,1)S(1)}, bf16[128,1,16,512]{0,3,2,1:T(8,128)(2,1)}) fusion(bf16[128,2,16,512]{0,3,2,1:T(8,128)(2,1)} %bitcast.11), kind=kLoop, calls=%fused_computation.32 | loop fusion | bytes 8388608 | tf_op jit(solution)/shard_map/slice | solution.py:79
  140.4 4.6 %copy.29 = bf16[128,1,16,512]{3,2,0,1:T(8,128)(2,1)} copy(bf16[128,1,16,512]{0,3,2,1:T(8,128)(2,1)} %get-tuple-element.125) | data formatting | bytes 4194304 | tf_op jit(solution)/shard_map/slice | solution.py:78
  145.0 42.1 %while.22 = (s32[]{:T(128)}, f32[8,512,16]{1,2,0:T(8,128)}, bf16[8,512,512]{2,1,0:T(8,128)(2,1)}, bf16[2048,512]{1,0:T(8,128)(2,1)}, s32[8,512]{1,0:T(8,128)S(1)}, /*index=5*/s32[]{:T(128)}) while((s32[]{:T(128)}, f32[8,512,16]{1,2,0:T(8,128)}, bf16[8,512,512]{2,1,0:T(8,128)(2,1)}, bf16[2048,512]{1,0:T(8,128)(2,1)}, ...), condition=%wide.region_2.3_spmd.clone, body=%wide.region_0.2_spmd.clone.sunk | while | flops 1075961856 | bytes 3251273 | solution.py:95
  145.0 4.6 %multiply_reduce_fusion.2 = f32[512,16]{0,1:T(8,128)S(1)} fusion(bf16[128,16,512]{2,1,0:T(8,128)(2,1)} %bitcast.77, f32[512,128]{0,1:T(8,128)S(1)} %fusion.37, bf16[8,512,512]{2,1,0:T(8,128)(2,1)} %get-tuple-element.208, s32[]{:T(128)} %get-tuple-element.200), kind=kOutput, calls=%fused_computation.2.clone.1 | convolution fusion | flops 1075830784 | bytes 2916864 | tf_op jit(solution)/shard_map/while/body/eval_jaxpr/te,ke->tk/dot_general | solution.py:92
  149.6 0.6 bitcast_dynamic-update-slice_fusion.2
  150.3 4.6 %multiply_reduce_fusion.2 = f32[512,16]{0,1:T(8,128)S(1)} fusion(bf16[128,16,512]{2,1,0:T(8,128)(2,1)} %bitcast.77, f32[512,128]{0,1:T(8,128)S(1)} %fusion.37, bf16[8,512,512]{2,1,0:T(8,128)(2,1)} %get-tuple-element.208, s32[]{:T(128)} %get-tuple-element.200), kind=kOutput, calls=%fused_computation.2.clone.1 | convolution fusion | flops 1075830784 | bytes 2916864 | tf_op jit(solution)/shard_map/while/body/eval_jaxpr/te,ke->tk/dot_general | solution.py:92
  154.9 0.6 bitcast_dynamic-update-slice_fusion.2
  155.6 4.6 %multiply_reduce_fusion.2 = f32[512,16]{0,1:T(8,128)S(1)} fusion(bf16[128,16,512]{2,1,0:T(8,128)(2,1)} %bitcast.77, f32[512,128]{0,1:T(8,128)S(1)} %fusion.37, bf16[8,512,512]{2,1,0:T(8,128)(2,1)} %get-tuple-element.208, s32[]{:T(128)} %get-tuple-element.200), kind=kOutput, calls=%fused_computation.2.clone.1 | convolution fusion | flops 1075830784 | bytes 2916864 | tf_op jit(solution)/shard_map/while/body/eval_jaxpr/te,ke->tk/dot_general | solution.py:92
  160.2 0.6 bitcast_dynamic-update-slice_fusion.2
  160.8 4.6 %multiply_reduce_fusion.2 = f32[512,16]{0,1:T(8,128)S(1)} fusion(bf16[128,16,512]{2,1,0:T(8,128)(2,1)} %bitcast.77, f32[512,128]{0,1:T(8,128)S(1)} %fusion.37, bf16[8,512,512]{2,1,0:T(8,128)(2,1)} %get-tuple-element.208, s32[]{:T(128)} %get-tuple-element.200), kind=kOutput, calls=%fused_computation.2.clone.1 | convolution fusion | flops 1075830784 | bytes 2916864 | tf_op jit(solution)/shard_map/while/body/eval_jaxpr/te,ke->tk/dot_general | solution.py:92
  165.4 0.6 bitcast_dynamic-update-slice_fusion.2
  166.1 4.6 %multiply_reduce_fusion.2 = f32[512,16]{0,1:T(8,128)S(1)} fusion(bf16[128,16,512]{2,1,0:T(8,128)(2,1)} %bitcast.77, f32[512,128]{0,1:T(8,128)S(1)} %fusion.37, bf16[8,512,512]{2,1,0:T(8,128)(2,1)} %get-tuple-element.208, s32[]{:T(128)} %get-tuple-element.200), kind=kOutput, calls=%fused_computation.2.clone.1 | convolution fusion | flops 1075830784 | bytes 2916864 | tf_op jit(solution)/shard_map/while/body/eval_jaxpr/te,ke->tk/dot_general | solution.py:92
  170.7 0.6 bitcast_dynamic-update-slice_fusion.2
  171.4 4.6 %multiply_reduce_fusion.2 = f32[512,16]{0,1:T(8,128)S(1)} fusion(bf16[128,16,512]{2,1,0:T(8,128)(2,1)} %bitcast.77, f32[512,128]{0,1:T(8,128)S(1)} %fusion.37, bf16[8,512,512]{2,1,0:T(8,128)(2,1)} %get-tuple-element.208, s32[]{:T(128)} %get-tuple-element.200), kind=kOutput, calls=%fused_computation.2.clone.1 | convolution fusion | flops 1075830784 | bytes 2916864 | tf_op jit(solution)/shard_map/while/body/eval_jaxpr/te,ke->tk/dot_general | solution.py:92
  176.0 0.6 bitcast_dynamic-update-slice_fusion.2
  176.6 4.6 %multiply_reduce_fusion.2 = f32[512,16]{0,1:T(8,128)S(1)} fusion(bf16[128,16,512]{2,1,0:T(8,128)(2,1)} %bitcast.77, f32[512,128]{0,1:T(8,128)S(1)} %fusion.37, bf16[8,512,512]{2,1,0:T(8,128)(2,1)} %get-tuple-element.208, s32[]{:T(128)} %get-tuple-element.200), kind=kOutput, calls=%fused_computation.2.clone.1 | convolution fusion | flops 1075830784 | bytes 2916864 | tf_op jit(solution)/shard_map/while/body/eval_jaxpr/te,ke->tk/dot_general | solution.py:92
  181.3 0.6 bitcast_dynamic-update-slice_fusion.2
  181.9 4.6 %multiply_reduce_fusion.2 = f32[512,16]{0,1:T(8,128)S(1)} fusion(bf16[128,16,512]{2,1,0:T(8,128)(2,1)} %bitcast.77, f32[512,128]{0,1:T(8,128)S(1)} %fusion.37, bf16[8,512,512]{2,1,0:T(8,128)(2,1)} %get-tuple-element.208, s32[]{:T(128)} %get-tuple-element.200), kind=kOutput, calls=%fused_computation.2.clone.1 | convolution fusion | flops 1075830784 | bytes 2916864 | tf_op jit(solution)/shard_map/while/body/eval_jaxpr/te,ke->tk/dot_general | solution.py:92
  186.5 0.6 bitcast_dynamic-update-slice_fusion.2
  187.2 3.1 %copy.30 = bf16[128,1,16,512]{3,2,0,1:T(8,128)(2,1)} copy(bf16[128,1,16,512]{0,3,2,1:T(8,128)(2,1)S(1)} %get-tuple-element.124) | data formatting | bytes 4194304 | tf_op jit(solution)/shard_map/slice | solution.py:79
  190.2 31.1 %all-gather.3.cloned.1.call-done = f32[128,512,16]{1,2,0:T(8,128)} async-done(((f32[8,512,16]{1,2,0:T(8,128)}), f32[128,512,16]{1,2,0:T(8,128)}) %all-gather.3.cloned.1.call-update) | async-done | bytes 4194320 | tf_op jit(solution)/shard_map/all_gather | solution.py:30
  221.3 2.6 reduce_sum.18
  224.0 31.9 %while.23 = (s32[]{:T(128)}, bf16[8,512,512]{2,1,0:T(8,128)(2,1)}, bf16[8,512,512]{2,1,0:T(8,128)(2,1)}, s32[8,512]{1,0:T(8,128)S(1)}, bf16[8,512,16]{1,2,0:T(8,...) while((s32[]{:T(128)}, bf16[8,512,512]{2,1,0:T(8,128)(2,1)}, bf16[8,512,512]{2,1,0:T(8,128)(2,1)}, ...), condition=%wide.region_5.6_spmd.clone, body=%wide.region_4.5_spmd.clone.sunk | while | flops 1075970048 | bytes 7658069 | solution.py:108
  224.1 0.2 broadcast_multiply_fusion.2
  224.3 3.7 %fusion.41 = bf16[8,512,512]{2,1,0:T(8,128)(2,1)} fusion(bf16[8,512,512]{2,1,0:T(8,128)(2,1)} %get-tuple-element.220, s32[]{:T(128)} %get-tuple-element.219, bf16[512,2048]{0,1:T(8,128)(2,1)S(1)} %bitcast.71, bf16[2048,512]{1,0:T(8,128)(2,1)} %get-tuple-element.231, bf16[8,512,512]{2,1,0:T(8,128)(2,1)} %get-tuple-element.228), kind=kOutput, calls=%fused_computation.15.clone.1 | convolution fusion | flops 1074790400 | bytes 5243392 | tf_op jit(solution)/shard_map/while/body/eval_jaxpr/dot_general | solution.py:103
  228.1 0.2 broadcast_multiply_fusion.2
  228.3 3.7 %fusion.41 = bf16[8,512,512]{2,1,0:T(8,128)(2,1)} fusion(bf16[8,512,512]{2,1,0:T(8,128)(2,1)} %get-tuple-element.220, s32[]{:T(128)} %get-tuple-element.219, bf16[512,2048]{0,1:T(8,128)(2,1)S(1)} %bitcast.71, bf16[2048,512]{1,0:T(8,128)(2,1)} %get-tuple-element.231, bf16[8,512,512]{2,1,0:T(8,128)(2,1)} %get-tuple-element.228), kind=kOutput, calls=%fused_computation.15.clone.1 | convolution fusion | flops 1074790400 | bytes 5243392 | tf_op jit(solution)/shard_map/while/body/eval_jaxpr/dot_general | solution.py:103
  232.1 0.2 broadcast_multiply_fusion.2
  232.2 3.7 %fusion.41 = bf16[8,512,512]{2,1,0:T(8,128)(2,1)} fusion(bf16[8,512,512]{2,1,0:T(8,128)(2,1)} %get-tuple-element.220, s32[]{:T(128)} %get-tuple-element.219, bf16[512,2048]{0,1:T(8,128)(2,1)S(1)} %bitcast.71, bf16[2048,512]{1,0:T(8,128)(2,1)} %get-tuple-element.231, bf16[8,512,512]{2,1,0:T(8,128)(2,1)} %get-tuple-element.228), kind=kOutput, calls=%fused_computation.15.clone.1 | convolution fusion | flops 1074790400 | bytes 5243392 | tf_op jit(solution)/shard_map/while/body/eval_jaxpr/dot_general | solution.py:103
  236.1 0.2 broadcast_multiply_fusion.2
  236.2 3.7 %fusion.41 = bf16[8,512,512]{2,1,0:T(8,128)(2,1)} fusion(bf16[8,512,512]{2,1,0:T(8,128)(2,1)} %get-tuple-element.220, s32[]{:T(128)} %get-tuple-element.219, bf16[512,2048]{0,1:T(8,128)(2,1)S(1)} %bitcast.71, bf16[2048,512]{1,0:T(8,128)(2,1)} %get-tuple-element.231, bf16[8,512,512]{2,1,0:T(8,128)(2,1)} %get-tuple-element.228), kind=kOutput, calls=%fused_computation.15.clone.1 | convolution fusion | flops 1074790400 | bytes 5243392 | tf_op jit(solution)/shard_map/while/body/eval_jaxpr/dot_general | solution.py:103
  240.0 0.2 broadcast_multiply_fusion.2
  240.2 3.8 %fusion.41 = bf16[8,512,512]{2,1,0:T(8,128)(2,1)} fusion(bf16[8,512,512]{2,1,0:T(8,128)(2,1)} %get-tuple-element.220, s32[]{:T(128)} %get-tuple-element.219, bf16[512,2048]{0,1:T(8,128)(2,1)S(1)} %bitcast.71, bf16[2048,512]{1,0:T(8,128)(2,1)} %get-tuple-element.231, bf16[8,512,512]{2,1,0:T(8,128)(2,1)} %get-tuple-element.228), kind=kOutput, calls=%fused_computation.15.clone.1 | convolution fusion | flops 1074790400 | bytes 5243392 | tf_op jit(solution)/shard_map/while/body/eval_jaxpr/dot_general | solution.py:103
  244.0 0.2 broadcast_multiply_fusion.2
  244.2 3.7 %fusion.41 = bf16[8,512,512]{2,1,0:T(8,128)(2,1)} fusion(bf16[8,512,512]{2,1,0:T(8,128)(2,1)} %get-tuple-element.220, s32[]{:T(128)} %get-tuple-element.219, bf16[512,2048]{0,1:T(8,128)(2,1)S(1)} %bitcast.71, bf16[2048,512]{1,0:T(8,128)(2,1)} %get-tuple-element.231, bf16[8,512,512]{2,1,0:T(8,128)(2,1)} %get-tuple-element.228), kind=kOutput, calls=%fused_computation.15.clone.1 | convolution fusion | flops 1074790400 | bytes 5243392 | tf_op jit(solution)/shard_map/while/body/eval_jaxpr/dot_general | solution.py:103
  248.2 3.8 %fusion.41 = bf16[8,512,512]{2,1,0:T(8,128)(2,1)} fusion(bf16[8,512,512]{2,1,0:T(8,128)(2,1)} %get-tuple-element.220, s32[]{:T(128)} %get-tuple-element.219, bf16[512,2048]{0,1:T(8,128)(2,1)S(1)} %bitcast.71, bf16[2048,512]{1,0:T(8,128)(2,1)} %get-tuple-element.231, bf16[8,512,512]{2,1,0:T(8,128)(2,1)} %get-tuple-element.228), kind=kOutput, calls=%fused_computation.15.clone.1 | convolution fusion | flops 1074790400 | bytes 5243392 | tf_op jit(solution)/shard_map/while/body/eval_jaxpr/dot_general | solution.py:103
  252.2 3.8 %fusion.41 = bf16[8,512,512]{2,1,0:T(8,128)(2,1)} fusion(bf16[8,512,512]{2,1,0:T(8,128)(2,1)} %get-tuple-element.220, s32[]{:T(128)} %get-tuple-element.219, bf16[512,2048]{0,1:T(8,128)(2,1)S(1)} %bitcast.71, bf16[2048,512]{1,0:T(8,128)(2,1)} %get-tuple-element.231, bf16[8,512,512]{2,1,0:T(8,128)(2,1)} %get-tuple-element.228), kind=kOutput, calls=%fused_computation.15.clone.1 | convolution fusion | flops 1074790400 | bytes 5243392 | tf_op jit(solution)/shard_map/while/body/eval_jaxpr/dot_general | solution.py:103
  255.9 1.6 copy-done.1
  (60 shorter events, 1.2 us)
Async XLA Ops:
  6.5 34.8 %copy-start = (bf16[1024,1024]{1,0:T(8,128)(2,1)S(1)}, bf16[1024,1024]{1,0:T(8,128)(2,1)}, u32[]{:S(2)}) copy-start(bf16[1024,1024]{1,0:T(8,128)(2,1)} %param.14) | copy-start | bytes 6291460
  7.9 33.3 %all-to-all-start = ((s32[8,1,128]{2,1,0:T(1,128)}), s32[8,1,128]{2,1,0:T(1,128)S(1)}, u32[]{:S(2)}, u32[]{:S(2)}) async-start(s32[8,1,128]{2,1,0:T(1,128)} %broadcast_in_dim.18), calls=%async_computation | async-start | bytes 8192 | tf_op jit(solution)/shard_map/all_to_all | solution.py:20
  28.6 12.5 %copy-start.3 = (f32[2048]{0:T(1024)S(1)}, f32[2048]{0:T(1024)}, u32[]{:S(2)}) copy-start(f32[2048]{0:T(1024)} %param.18) | copy-start | bytes 24580
  28.6 12.7 %copy-start.4 = (f32[2048]{0:T(1024)S(1)}, f32[2048]{0:T(1024)}, u32[]{:S(2)}) copy-start(f32[2048]{0:T(1024)} %param.16) | copy-start | bytes 24580
  73.0 11.1 %copy-start.2 = (s32[4096]{0:T(1024)S(1)}, s32[4096]{0:T(1024)}, u32[]{:S(2)}) copy-start(s32[4096]{0:T(1024)} %param.19) | copy-start | bytes 49156
  73.0 63.4 %all-to-all-start.1 = ((bf16[128,128,128]{0,2,1:T(8,128)(2,1)}), bf16[128,128,128]{0,2,1:T(8,128)(2,1)}, u32[]{:S(2)}, u32[]{:S(2)}) async-start(bf16[128,128,128]{0,2,1:T(8,128)(2,1)} %copy.28), calls=%async_computation.1 | async-start | bytes 8388608 | tf_op jit(solution)/shard_map/all_to_all | solution.py:69
  83.8 137.5 %all-gather.3.cloned.1.call-start = ((), (), s32[]{:S(2)}) async-start(), calls=%async_computation.2 | async-start | bytes 4456448 | tf_op jit(solution)/shard_map/all_gather | solution.py:30
  255.9 1.6 copy-start.1
Sparse Core Ops, SparseCore 0:
  187.3 34.0 all-gather.2
where the time goes:
time: 266 us; the launch traced here: 264 us
  matrix products  92.2 us (35%)
  waiting for transfers between devices  83.4 us (31%)
  local copies, waits for them, and re-layouts  51.1 us (19%)
  starting transfers between devices  19.4 us (7%)
  between operations  13.5 us (5%)
  other arithmetic  4.5 us (2%)
    all_to_all x1, waiting for transfers between devices, on_device(): lax.all_to_all(factors.reshape(rows_dev, task_count * width_count, inner_...  52.3 us
    dot_general x8, matrix products, rank_block(): jnp.einsum('te,ke->tk', tokens_in, entry_flat, preferred_element_type=jnp...  36.9 us
    all_gather x1, waiting for transfers between devices, total_of_pieces(): tiles = lax.all_gather(shard, axis)  31.1 us
    dot_general x8, matrix products, update_block(): update = jnp.dot(spread, exit_flat, preferred_element_type=jnp.float32)  30 us
    unnamed x11, local copies, waits for them, and re-layouts  14 us
    dot_general x1, matrix products, on_device(): jnp.einsum('tqh,hks->qtsk', hidden_rows, weight_cube, preferred_element_t...  13.8 us
    reshape x1, local copies, waits for them, and re-layouts, on_device(): head_weight.reshape(head_weight.shape[0], inner_cols, width_count)  12.5 us
    dot_general x1, matrix products, run_trunk(): jnp.dot(embedded, trunk_weight, preferred_element_type=jnp.float32)  11.5 us
  transfers between devices with their start and end apart: 3, of which 2 were waited for; matrix products, arithmetic and copies ran while one was open for 11% of the time, Pallas kernels for 0%

commit v1 on v0

v1 whole, which is shorter than its diff:
```python
import math

import jax
import jax.numpy as jnp
from jax import lax
from jax.experimental import pallas as pl
from jax.experimental.pallas import tpu as pltpu
from jax.sharding import PartitionSpec as P

WIDTH = 8192
RANK = 16
LANES = 128
BOTH = ("task", "width")
BF16 = jnp.bfloat16
F32 = jnp.float32


def product(a, b, a_dim=1, b_dim=0):
    return lax.dot_general(a, b, (((a_dim,), (b_dim,)), ((), ())), preferred_element_type=F32)


def iota(shape, dim):
    return lax.broadcasted_iota(jnp.int32, shape, dim)


def one_where(test):
    return jnp.where(test, 1.0, 0.0).astype(BF16)


def lane_group(rows):
    return (iota((rows, LANES), 1) >> 4).astype(F32).astype(BF16)


def cost(flops, moved):
    return pl.CostEstimate(flops=int(flops), transcendentals=0, bytes_accessed=int(moved))


def head_kernel(low_ref, high_ref, weight_ref, bias_ref, out_ref):
    step = pl.program_id(0)
    half = low_ref.shape[1]
    out = product(low_ref[...], weight_ref[:half, :])
    out = out + product(high_ref[...], weight_ref[half:, :]) + bias_ref[...]
    col = iota((256, 256), 0)
    target = ((col >> 3) & 1) * 128 + ((step + col) & 7) * 16 + (col >> 4)
    perm = one_where(iota((256, 256), 1) == target)
    grouped = product(out.astype(BF16), perm).astype(BF16)
    group = iota((1, LANES), 1) >> 4
    for turn in range(8):
        here = jnp.broadcast_to(one_where(group == ((step + turn) & 7)), (16, LANES)) > 0.5
        for side in range(2):
            dest = side * 8 + turn
            for at in range(0, out.shape[0], 16):
                new = grouped[at : at + 16, side * LANES : side * LANES + LANES]
                out_ref[dest, at : at + 16] = jnp.where(here, new, out_ref[dest, at : at + 16])


def table_factors(low, high, head_weight, bias):
    entries, half = low.shape
    hid, cols = head_weight.shape
    return pl.pallas_call(
        head_kernel,
        grid=(cols // 256,),
        in_specs=[
            pl.BlockSpec((entries, half), lambda i: (0, 0)),
            pl.BlockSpec((entries, half), lambda i: (0, 0)),
            pl.BlockSpec((hid, 256), lambda i: (0, i)),
            pl.BlockSpec((1, 256), lambda i: (0, i)),
        ],
        out_specs=pl.BlockSpec((16, entries, LANES), lambda i: (0, 0, 0)),
        out_shape=jax.ShapeDtypeStruct((16, entries, LANES), BF16),
        cost_estimate=cost(2 * entries * cols * (hid + 256), 2 * hid * cols),
        name="head",
    )(low, high, head_weight, bias)


def pick_kernel(me_ref, id_ref, table_ref, out_ref, hot_ref):
    step = pl.program_id(0)
    tasks, rows, _ = id_ref.shape
    entries = table_ref.shape[1]

    @pl.when(step == 0)
    def _():
        lane = iota((rows, LANES), 1)
        for task in range(tasks):
            ids = id_ref[task ^ me_ref[0]]
            for at in range(0, entries, LANES):
                hot_ref[task * rows : (task + 1) * rows, at : at + LANES] = one_where(
                    ids == lane + at
                )

    pair = jnp.concatenate([table_ref[0], table_ref[1]], axis=1)
    picked = product(hot_ref[...], pair)
    for side in range(2):
        turn = (2 * step + side) & 7
        piece = pltpu.roll(picked[:, side * LANES : side * LANES + LANES], (8 - turn) * 16, 1)
        out_ref[:, side] = piece.astype(BF16).reshape(tasks, rows, LANES)


def picked_rows(me, ids, factors):
    tasks, rows = ids.shape
    dests, entries, _ = factors.shape
    id_grid = jnp.broadcast_to(ids[:, :, None], (tasks, rows, LANES))
    return pl.pallas_call(
        pick_kernel,
        grid=(dests // 2,),
        in_specs=[
            pl.BlockSpec(memory_space=pltpu.SMEM),
            pl.BlockSpec((tasks, rows, LANES), lambda i: (0, 0, 0)),
            pl.BlockSpec((2, entries, LANES), lambda i: (i, 0, 0)),
        ],
        out_specs=pl.BlockSpec((tasks, 2, rows, LANES), lambda i: (0, i, 0, 0)),
        out_shape=jax.ShapeDtypeStruct((tasks, dests, rows, LANES), BF16),
        scratch_shapes=[pltpu.VMEM((tasks * rows, entries), BF16)],
        cost_estimate=cost(2 * tasks * rows * entries * dests * LANES, 8 << 20),
        name="pick",
    )(me, id_grid, factors)


def sort_kernel(all_ref, row_ref, in_ref, out_ref, low_ref, part_ref, name_ref, rank_ref, slot_ref):
    step = pl.program_id(0)
    tokens = all_ref.shape[1]
    tile = out_ref.shape[0]
    count = 128
    per_row = tokens // count

    @pl.when(step == 0)
    def _():
        before = one_where(iota((256, 256), 0) < iota((256, 256), 1))
        carry = jnp.zeros((count, 1), F32)
        for at in range(0, tokens, 256):
            rows = all_ref[:, at : at + 256]
            hot = jnp.where(iota((count, 256), 0) == rows, 1.0, 0.0)
            seen = product(hot.astype(BF16), before) + carry
            rank = jnp.sum(hot * seen, axis=0, keepdims=True).astype(jnp.int32)
            carry = carry + jnp.sum(hot, axis=1, keepdims=True)
            slot = rows * per_row + rank
            slot_ref[:, at : at + 256] = slot
            rank_ref[at // 256] = slot

    total = jnp.zeros(out_ref.shape, F32)
    for at in range(0, tokens, 1024):
        place = iota((tile, 1024), 0) + step * tile
        hot = one_where(place == slot_ref[:, at : at + 1024])
        total = total + product(hot, in_ref[at : at + 1024, :])
    out_ref[...] = total.astype(BF16)

    for at in range(0, tile, 256):
        slot = rank_ref[step * (tile // 256) + at // 256]
        slot = jnp.broadcast_to(slot.astype(F32), (LANES, 256)).T.astype(jnp.int32)
        span = slice(at, at + 256)
        lane = iota((256, LANES), 1)
        low_ref[span, :LANES] = one_where((slot & 255) == lane)
        low_ref[span, LANES:] = one_where((slot & 255) == lane + LANES)
        part_ref[span, :] = (slot >> 8).astype(F32).astype(BF16)
        name_ref[span, :] = (slot // per_row).astype(F32).astype(BF16)


def sorted_tokens(local_row, inputs):
    tokens, width = inputs.shape
    tile = 512
    wide = lambda lanes: jax.ShapeDtypeStruct((tokens, lanes), BF16)
    return pl.pallas_call(
        sort_kernel,
        grid=(tokens // tile,),
        in_specs=[
            pl.BlockSpec((1, tokens), lambda i: (0, 0)),
            pl.BlockSpec((1, tile), lambda i: (0, i)),
            pl.BlockSpec((tokens, width), lambda i: (0, 0)),
        ],
        out_specs=[
            pl.BlockSpec((tile, width), lambda i: (i, 0)),
            pl.BlockSpec((tile, 256), lambda i: (i, 0)),
            pl.BlockSpec((tile, LANES), lambda i: (i, 0)),
            pl.BlockSpec((tile, LANES), lambda i: (i, 0)),
        ],
        out_shape=[wide(width), wide(256), wide(LANES), wide(LANES)],
        scratch_shapes=[
            pltpu.VMEM((tokens // 256, 1, 256), jnp.int32),
            pltpu.VMEM((1, tokens), jnp.int32),
        ],
        cost_estimate=cost(2 * tokens * tokens * width, 16 << 20),
        name="sort",
    )(local_row, local_row, inputs)


def entry_kernel(in_ref, block_ref, out_ref):
    slots = in_ref.shape[0]
    part = block_ref.shape[3]
    factor = jnp.concatenate(
        [block_ref[0, :, q].reshape(RANK * part, LANES) for q in range(4)], axis=1
    )
    scores = product(factor, in_ref[...], 1, 1).reshape(RANK, part, slots)
    match = iota((part, slots), 0) == iota((part, slots), 1) // (slots // part)
    coef = jnp.sum(jnp.where(match[None], scores, 0.0), axis=1)
    for at in range(out_ref.shape[0]):
        out_ref[at] = coef[:, at * 256 : (at + 1) * 256]


def rank_parts(inputs, blocks):
    tokens, width = inputs.shape
    rows = blocks.shape[3]
    part = 16
    steps = rows // part
    tile = tokens // steps
    return pl.pallas_call(
        entry_kernel,
        grid=(steps,),
        in_specs=[
            pl.BlockSpec((tile, width), lambda i: (i, 0)),
            pl.BlockSpec((1, RANK, 4, part, LANES), lambda i: (0, 0, 0, i, 0)),
        ],
        out_specs=pl.BlockSpec((tile // 256, RANK, 256), lambda i: (i, 0, 0)),
        out_shape=jax.ShapeDtypeStruct((tokens // 256, RANK, 256), F32),
        name="entry",
    )(inputs, blocks)


def order_kernel(block_ref, out_ref):
    out_at = iota((256, 256), 0)
    perm = one_where(iota((256, 256), 1) == (out_at & 15) * 16 + (out_at >> 4))
    piece = jnp.concatenate(
        [block_ref[0, :, q].reshape(RANK * 16, LANES) for q in range(4)], axis=1
    )
    out_ref[...] = product(perm, piece).astype(BF16)


def ordered_exit(blocks):
    rows = blocks.shape[3]
    return pl.pallas_call(
        order_kernel,
        grid=(rows // 16,),
        in_specs=[pl.BlockSpec((1, RANK, 4, 16, LANES), lambda i: (1, 0, 0, i, 0))],
        out_specs=pl.BlockSpec((256, 4 * LANES), lambda i: (i, 0)),
        out_shape=jax.ShapeDtypeStruct((rows * RANK, 4 * LANES), BF16),
        name="order",
    )(blocks)


def exit_kernel(coef_ref, low_ref, part_ref, name_ref, base_ref, factor_ref, out_ref):
    tile = base_ref.shape[0]
    depth = factor_ref.shape[0]
    group = lane_group(tile)
    zero = jnp.zeros((tile, LANES), F32)
    values = product(low_ref[...], coef_ref[...], 1, 1)
    part = part_ref[...].astype(F32)
    group32 = group.astype(F32)
    mine = jnp.where(part == group32, values[:, :LANES], zero)
    mine = mine + jnp.where(part == group32 + 8.0, values[:, LANES:], zero)
    fold = one_where((iota((LANES, LANES), 0) & 15) == (iota((LANES, LANES), 1) & 15))
    coef = product(mine.astype(BF16), fold).astype(BF16)
    name = name_ref[...]
    spread = jnp.concatenate(
        [
            jnp.where(name == group + jnp.asarray(at, BF16), coef, jnp.zeros_like(coef))
            for at in range(0, depth // RANK, 8)
        ],
        axis=1,
    )
    update = product(spread, factor_ref[...])
    base = base_ref[...].astype(F32)
    out_ref[...] = (base + update * (1.0 / math.sqrt(RANK))).astype(BF16)


def apply_update(coefs, low, part, name, base, factors):
    tokens, width = base.shape
    tile = 512
    return pl.pallas_call(
        exit_kernel,
        grid=(tokens // tile,),
        in_specs=[
            pl.BlockSpec(coefs.shape, lambda i: (0, 0)),
            pl.BlockSpec((tile, 256), lambda i: (i, 0)),
            pl.BlockSpec((tile, LANES), lambda i: (i, 0)),
            pl.BlockSpec((tile, LANES), lambda i: (i, 0)),
            pl.BlockSpec((tile, width), lambda i: (i, 0)),
            pl.BlockSpec(factors.shape, lambda i: (0, 0)),
        ],
        out_specs=pl.BlockSpec((tile, width), lambda i: (i, 0)),
        out_shape=jax.ShapeDtypeStruct((tokens, width), BF16),
        name="exit",
    )(coefs, low, part, name, base, factors)


def to_all(shard, axis):
    length = lax.axis_size(axis)
    return lax.all_to_all(
        jnp.broadcast_to(shard[None], (length, *shard.shape)), axis, 0, 0, tiled=True
    )


def gathered(shard, axis):
    length = lax.axis_size(axis)
    held = shard[None]
    step = 1
    while step < length:
        moved = lax.ppermute(held, axis, [(at, at ^ step) for at in range(length)])
        held = jnp.concatenate([held, moved])
        step *= 2
    return held


def on_device(
    task_ids,
    embed_table,
    trunk_weight,
    trunk_bias,
    head_weight,
    head_bias,
    token_row,
    inputs,
    frozen,
):
    tasks = lax.axis_size("task")
    width = lax.axis_size("width")
    rows_dev = task_ids.shape[0]
    me = lax.axis_index("task")
    ids = gathered(task_ids, "task")

    half = trunk_weight.shape[1] // 2
    tables = []
    for cut in (slice(0, half), slice(half, 2 * half)):
        preact = jnp.dot(embed_table, trunk_weight[:, cut], preferred_element_type=F32)
        tables.append(jax.nn.silu(preact + trunk_bias[cut]).astype(BF16))
    factors = table_factors(*tables, head_weight, head_bias.reshape(1, -1))
    blocks = picked_rows(me.reshape(1), ids, factors)
    moved = lax.all_to_all(
        blocks.reshape(tasks * width, rows_dev, LANES), BOTH, 0, 0, tiled=True
    ).reshape(2, RANK, 4, rows_dev, LANES)

    local_row = (token_row - me * rows_dev).reshape(1, -1)
    in_order, low, part, name = sorted_tokens(local_row, inputs)
    parts = rank_parts(in_order, moved)
    pieces = lax.all_to_all(parts, "width", 0, 0, tiled=True)
    coef = (pieces.sum(axis=0) * (1.0 / math.sqrt(WIDTH))).astype(BF16)
    coefs = to_all(coef, "width").reshape(width * RANK, -1)
    return apply_update(coefs, low, part, name, frozen, ordered_exit(moved))


def solution(mesh):
    return jax.shard_map(
        on_device,
        mesh=mesh,
        in_specs=(
            P("task"),
            P(),
            P(),
            P(),
            P(None, BOTH),
            P(BOTH),
            P("task"),
            P("task", "width"),
            P("task", "width"),
        ),
        out_specs=P("task", "width"),
        check_vma=False,
    )
```

time: 266 us -> 157 us (0.59)
  Pallas kernels: 0 us -> 83.5 us
  matrix products: 92.2 us -> 9.92 us
  waiting for transfers between devices: 83.4 us -> 28.2 us
  local copies, waits for them, and re-layouts: 51.1 us -> 3.02 us
  between operations: 13.5 us -> 0.05 us
  blocking collectives: 0 us -> 11.5 us
  other arithmetic: 4.5 us -> 0.65 us
    pallas_call x0 -> x6, Pallas kernels: none -> 83.5 us  [the longest x1 23.7 us: sorted_tokens(): pl.pallas_call(sort_kernel, grid=(tokens // tile,), in_specs=[pl.BlockSpe...]
    dot_general x18 -> x2, matrix products: 92.2 us -> 9.92 us  [on_device(): jnp.dot(embed_table, trunk_weight[:, cut], preferred_element_type=F32)]
    all_gather x1 -> x0, waiting for transfers between devices: 31.1 us -> none  [total_of_pieces(): tiles = lax.all_gather(shard, axis)]
    all_to_all x2, waiting for transfers between devices: 52.3 us -> 28.2 us  [the longest x1 28.2 us: on_device(): lax.all_to_all(blocks.reshape(tasks * width, rows_dev, LANES), BOTH, 0, 0...]
    reshape x4 -> x0, local copies, waits for them, and re-layouts: 19 us -> none  [the longest x1 12.5 us: on_device(): head_weight.reshape(head_weight.shape[0], inner_cols, width_count)]
    unnamed x11 -> x10, local copies, waits for them, and re-layouts: 14 us -> 0.66 us
    all_to_all x0 -> x1, blocking collectives: none -> 11.5 us  [on_device(): pieces = lax.all_to_all(parts, 'width', 0, 0, tiled=True)]
    slice x3 -> x1, local copies, waits for them, and re-layouts: 11.7 us -> 0.7 us  [on_device(): tables.append(jax.nn.silu(preact + trunk_bias[cut]).astype(BF16))]
  transfers between devices with their start and end apart: 3 -> 5, of which waited for: 2 -> 1; matrix products, arithmetic and copies ran while one was open for 11% -> 7% of each run, Pallas kernels for 0% -> 32%
where the time goes in v1:
time: 157 us; the launch traced here: 156 us
  Pallas kernels  83.5 us (53%)
  waiting for transfers between devices  28.2 us (18%)
  starting transfers between devices  19 us (12%)
  blocking collectives  11.5 us (7%)
  matrix products  9.92 us (6%)
  local copies, waits for them, and re-layouts  3.02 us (2%)
    all_to_all x1, waiting for transfers between devices, on_device(): lax.all_to_all(blocks.reshape(tasks * width, rows_dev, LANES), BOTH, 0, 0...  28.2 us
    pallas_call x1, Pallas kernels, sorted_tokens(): pl.pallas_call(sort_kernel, grid=(tokens // tile,), in_specs=[pl.BlockSpe...  23.7 us
    pallas_call x1, Pallas kernels, table_factors(): pl.pallas_call(head_kernel, grid=(cols // 256,), in_specs=[pl.BlockSpec((...  19.9 us
    pallas_call x1, Pallas kernels, apply_update(): pl.pallas_call(exit_kernel, grid=(tokens // tile,), in_specs=[pl.BlockSpe...  15.9 us
    all_to_all x1, blocking collectives, on_device(): pieces = lax.all_to_all(parts, 'width', 0, 0, tiled=True)  11.5 us
    pallas_call x1, Pallas kernels, picked_rows(): pl.pallas_call(pick_kernel, grid=(dests // 2,), in_specs=[pl.BlockSpec(me...  10.4 us
    dot_general x2, matrix products, on_device(): jnp.dot(embed_table, trunk_weight[:, cut], preferred_element_type=F32)  9.92 us
    ppermute x3, starting transfers between devices, gathered(): moved = lax.ppermute(held, axis, [(at, at ^ step) for at in range(length)])  8.49 us
  transfers between devices with their start and end apart: 5, of which 1 were waited for; matrix products, arithmetic and copies ran while one was open for 7% of the time, Pallas kernels for 32%

profile of v1, /device:TPU:1, one launch (start us, length us, event | category | flops | bytes accessed | tf_op | source)
XLA Modules:
  0.0 155.9 jit_solution(17586248352512100451)
XLA Ops:
  0.0 0.0 copy-start
  0.0 4.4 %collective-permute-start = (s32[1,128]{1,0:T(1,128)}, s32[1,128]{1,0:T(1,128)S(1)}, u32[]{:S(2)}, u32[]{:S(2)}) collective-permute-start(s32[1,128]{1,0:T(1,128)} %bitcast.13), channel_id=1, source_target_pairs={{0,16},{16,0},{32,48},{48,32},{64,80},{80,64},{96,112},{112,96},{1... | collective-permute-start | bytes 1544 | tf_op jit(solution)/shard_map/ppermute | solution.py:296
  4.4 0.7 fusion.8
  5.1 0.0 copy-done
  5.1 0.0 copy-start.3
  5.1 0.0 copy-start.4
  5.1 5.8 %multiply_convert_fusion.high_ref = bf16[1024,1024]{1,0:T(8,128)(2,1)} fusion(f32[1024]{0:T(1024)S(1)} %get-tuple-element.13, bf16[1024,1024]{1,0:T(8,128)(2,1)S(1)} %copy-done, bf16[1024,2048]{1,0:T(8,128)(2,1)} %param.11), kind=kOutput, calls=%fused_computation | convolution fusion | flops 2153775104 | bytes 6295552 | tf_op jit(solution)/shard_map/dot_general | solution.py:322
  10.9 0.0 collective-permute-done
  10.9 0.0 copy-done.3
  10.9 1.4 collective-permute-start.1
  12.3 0.0 copy-done.4
  12.3 4.1 %multiply_convert_fusion.1.low_ref = bf16[1024,1024]{1,0:T(8,128)(2,1)} fusion(f32[1024]{0:T(1024)S(1)} %get-tuple-element.14, bf16[1024,1024]{1,0:T(8,128)(2,1)S(1)} %copy-done, bf16[1024,2048]{1,0:T(8,128)(2,1)S(1)} %copy-done.4), kind=kOutput, calls=%fused_computation.1 | convolution fusion | flops 2153775104 | bytes 6295552 | tf_op jit(solution)/shard_map/dot_general | solution.py:322
  16.4 0.0 collective-permute-done.1
  16.5 2.7 %collective-permute-start.2 = (s32[4,128]{1,0:T(4,128)S(1)}, s32[4,128]{1,0:T(4,128)S(1)}, u32[]{:S(2)}, u32[]{:S(2)}) collective-permute-start(s32[4,128]{1,0:T(4,128)S(1)} %pad_add_fusion.1), channel_id=1, source_target_pairs={{0,64},{16,80},{32,96},{48,112},{64,0},{80,16},{96,32},{112,48},{1... | collective-permute-start | bytes 6152 | tf_op jit(solution)/shard_map/ppermute | solution.py:296
  19.1 19.9 %head.1.table_ref = bf16[16,1024,128]{2,1,0:T(8,128)(2,1)} custom-call(bf16[1024,1024]{1,0:T(8,128)(2,1)} %multiply_convert_fusion.1.low_ref, bf16[1024,1024]{1,0:T(8,128)(2,1)} %multiply_convert_fusion.high_ref, bf16[2048,2048]{1,0:T(8,128)(2,1)} %weight_ref.1, f32[1,2048]{1,0:T(1,128)} %bitcast.17), custom_call_target="tpu_custom_call" | custom-call | flops 9663676416 | bytes 8388608 | tf_op jit(solution)/shard_map/head/pallas_call | solution.py:60
  39.0 0.0 collective-permute-done.2
  39.0 1.0 broadcast_in_dim.7.id_ref
  40.0 10.4 %pick.1 = bf16[8,16,128,128]{3,2,1,0:T(8,128)(2,1)} custom-call(s32[1]{0:T(128)} %bitcast.1.me_ref, s32[8,128,128]{2,1,0:T(8,128)} %broadcast_in_dim.7.id_ref, bf16[16,1024,128]{2,1,0:T(8,128)(2,1)} %head.1.table_ref), custom_call_target="tpu_custom_call" | custom-call | flops 4294967296 | bytes 8388608 | tf_op jit(solution)/shard_map/pick/pallas_call | solution.py:103
  50.4 0.0 copy-start.2
  50.4 6.4 %all-to-all-start = ((bf16[128,128,128]{2,1,0:T(8,128)(2,1)}), bf16[128,128,128]{2,1,0:T(8,128)(2,1)}, u32[]{:S(2)}, u32[]{:S(2)}) async-start(bf16[128,128,128]{2,1,0:T(8,128)(2,1)} %bitcast.9), calls=%async_computation | async-start | bytes 8388608 | tf_op jit(solution)/shard_map/all_to_all | solution.py:326
  56.8 0.0 copy-done.2
  56.8 0.6 broadcast_subtract_fusion
  57.4 23.7 %sort.1 = (bf16[4096,512]{1,0:T(8,128)(2,1)}, bf16[4096,256]{1,0:T(8,128)(2,1)}, bf16[4096,128]{1,0:T(8,128)(2,1)}, bf16[4096,128]{1,0:T(8,128)(2,1)}) custom-call(s32[1,4096]{1,0:T(1,128)} %bitcast.11, s32[1,4096]{1,0:T(1,128)} %bitcast.12, bf16[4096,512]{1,0:T(8,128)(2,1)} %in_ref.1), custom_call_target="tpu_custom_call" | custom-call | flops 17179869184 | bytes 16777216 | tf_op jit(solution)/shard_map/sort/pallas_call | solution.py:162
  81.1 28.2 %all-to-all-done = bf16[128,128,128]{2,1,0:T(8,128)(2,1)} async-done(((bf16[128,128,128]{2,1,0:T(8,128)(2,1)}), bf16[128,128,128]{2,1,0:T(8,128)(2,1)}, u32[]{:S(2)}, u32[]{:S(2)}) %all-to-all-start) | async-done | bytes 4194336 | tf_op jit(solution)/shard_map/all_to_all | solution.py:326
  109.4 7.3 %entry.1 = f32[16,16,256]{2,1,0:T(8,128)} custom-call(bf16[4096,512]{1,0:T(8,128)(2,1)} %get-tuple-element.9.in_ref, bf16[2,16,4,128,128]{4,3,2,1,0:T(8,128)(2,1)} %bitcast.5.block_ref), custom_call_target="tpu_custom_call" | custom-call | tf_op jit(solution)/shard_map/entry/pallas_call | solution.py:205
  116.6 11.5 %all_to_all.15 = f32[16,16,256]{2,1,0:T(8,128)S(1)} all-to-all(f32[16,16,256]{2,1,0:T(8,128)} %entry.1), channel_id=1, replica_groups=mesh['task'=8,'width'=16] {'width'}, dimensions={0} | all-to-all | bytes 524288 | tf_op jit(solution)/shard_map/all_to_all | solution.py:333
  128.2 0.7 broadcast_in_dim.8
  128.9 4.1 %all-to-all-start.2 = ((bf16[16,16,256]{2,1,0:T(8,128)(2,1)}), bf16[16,16,256]{2,1,0:T(8,128)(2,1)S(1)}, u32[]{:S(2)}, u32[]{:S(2)}) async-start(bf16[16,16,256]{2,1,0:T(8,128)(2,1)} %broadcast_in_dim.8), calls=%async_computation.2 | async-start | bytes 262144 | tf_op jit(solution)/shard_map/all_to_all | solution.py:286
  132.9 6.4 %order.1.factor_ref = bf16[2048,512]{1,0:T(8,128)(2,1)} custom-call(bf16[2,16,4,128,128]{4,3,2,1,0:T(8,128)(2,1)} %bitcast.5.block_ref), custom_call_target="tpu_custom_call" | custom-call | tf_op jit(solution)/shard_map/order/pallas_call | solution.py:229
  139.4 0.0 all-to-all-done.2
  139.4 0.0 copy-start.1
  139.4 0.6 copy-done.1
  140.0 15.9 %exit.1 = bf16[4096,512]{1,0:T(8,128)(2,1)} custom-call(bf16[256,256]{1,0:T(8,128)(2,1)} %bitcast.10, bf16[4096,256]{1,0:T(8,128)(2,1)} %get-tuple-element.10.low_ref, bf16[4096,128]{1,0:T(8,128)(2,1)} %get-tuple-element.11.part_ref, bf16[4096,128]{1,0:T(8,128)(2,1)} %get-tuple-element.12.name_ref, bf16[4096,512]{1,0:T(8,128)(2,1)} %base_ref.1, ...), custom_call_target="tpu_custom_call" | custom-call | tf_op jit(solution)/shard_map/exit/pallas_call | solution.py:267
  (5 shorter events, 0.1 us)
Async XLA Ops:
  0.0 5.1 %copy-start = (bf16[1024,1024]{1,0:T(8,128)(2,1)S(1)}, bf16[1024,1024]{1,0:T(8,128)(2,1)}, u32[]{:S(2)}) copy-start(bf16[1024,1024]{1,0:T(8,128)(2,1)} %param.10) | copy-start | bytes 6291460
  0.0 10.9 %collective-permute-start = (s32[1,128]{1,0:T(1,128)}, s32[1,128]{1,0:T(1,128)S(1)}, u32[]{:S(2)}, u32[]{:S(2)}) collective-permute-start(s32[1,128]{1,0:T(1,128)} %bitcast.13), channel_id=1, source_target_pairs={{0,16},{16,0},{32,48},{48,32},{64,80},{80,64},{96,112},{112,96},{1... | collective-permute-start | bytes 1544 | tf_op jit(solution)/shard_map/ppermute | solution.py:296
  5.1 5.8 %copy-start.3 = (s32[128]{0:T(128)S(1)}, s32[128]{0:T(128)}, u32[]{:S(2)}) copy-start(s32[128]{0:T(128)} %param.9) | copy-start | bytes 1540
  5.1 7.2 %copy-start.4 = (bf16[1024,2048]{1,0:T(8,128)(2,1)S(1)}, bf16[1024,2048]{1,0:T(8,128)(2,1)}, u32[]{:S(2)}) copy-start(bf16[1024,2048]{1,0:T(8,128)(2,1)} %param.11) | copy-start | bytes 12582916
  10.9 5.5 %collective-permute-start.1 = (s32[2,128]{1,0:T(2,128)S(1)}, s32[2,128]{1,0:T(2,128)S(1)}, u32[]{:S(2)}, u32[]{:S(2)}) collective-permute-start(s32[2,128]{1,0:T(2,128)S(1)} %pad_add_fusion.2), channel_id=1, source_target_pairs={{0,32},{16,48},{32,0},{48,16},{64,96},{80,112},{96,64},{112,80},{1... | collective-permute-start | bytes 3080 | tf_op jit(solution)/shard_map/ppermute | solution.py:296
  16.5 22.6 %collective-permute-start.2 = (s32[4,128]{1,0:T(4,128)S(1)}, s32[4,128]{1,0:T(4,128)S(1)}, u32[]{:S(2)}, u32[]{:S(2)}) collective-permute-start(s32[4,128]{1,0:T(4,128)S(1)} %pad_add_fusion.1), channel_id=1, source_target_pairs={{0,64},{16,80},{32,96},{48,112},{64,0},{80,16},{96,32},{112,48},{1... | collective-permute-start | bytes 6152 | tf_op jit(solution)/shard_map/ppermute | solution.py:296
  50.4 6.4 %copy-start.2 = (s32[4096]{0:T(1024)S(1)}, s32[4096]{0:T(1024)}, u32[]{:S(2)}) copy-start(s32[4096]{0:T(1024)} %param.15) | copy-start | bytes 49156
  50.4 59.0 %all-to-all-start = ((bf16[128,128,128]{2,1,0:T(8,128)(2,1)}), bf16[128,128,128]{2,1,0:T(8,128)(2,1)}, u32[]{:S(2)}, u32[]{:S(2)}) async-start(bf16[128,128,128]{2,1,0:T(8,128)(2,1)} %bitcast.9), calls=%async_computation | async-start | bytes 8388608 | tf_op jit(solution)/shard_map/all_to_all | solution.py:326
  128.9 10.5 %all-to-all-start.2 = ((bf16[16,16,256]{2,1,0:T(8,128)(2,1)}), bf16[16,16,256]{2,1,0:T(8,128)(2,1)S(1)}, u32[]{:S(2)}, u32[]{:S(2)}) async-start(bf16[16,16,256]{2,1,0:T(8,128)(2,1)} %broadcast_in_dim.8), calls=%async_computation.2 | async-start | bytes 262144 | tf_op jit(solution)/shard_map/all_to_all | solution.py:286
  139.4 0.6 copy-start.1

commit v2 on v1

v2 whole, which is shorter than its diff:
```python
import math

import jax
import jax.numpy as jnp
from jax import lax
from jax.experimental import pallas as pl
from jax.experimental.pallas import tpu as pltpu
from jax.sharding import PartitionSpec as P

WIDTH = 8192
RANK = 16
LANES = 128
BOTH = ("task", "width")
BF16 = jnp.bfloat16
F32 = jnp.float32


def product(a, b, a_dim=1, b_dim=0):
    return lax.dot_general(a, b, (((a_dim,), (b_dim,)), ((), ())), preferred_element_type=F32)


def iota(shape, dim):
    return lax.broadcasted_iota(jnp.int32, shape, dim)


def one_where(test):
    return jnp.where(test, 1.0, 0.0).astype(BF16)


def lane_group(rows):
    return (iota((rows, LANES), 1) >> 4).astype(F32).astype(BF16)


def cost(flops, moved):
    return pl.CostEstimate(flops=int(flops), transcendentals=0, bytes_accessed=int(moved))


def table_kernel(
    embed_ref, trunk_ref, trunk_bias_ref, weight_ref, bias_ref, out_ref, hidden_ref, group_ref
):
    step = pl.program_id(0)
    entries = embed_ref.shape[0]
    hid = hidden_ref.shape[1]
    wide = trunk_ref.shape[1]
    early = hid // wide
    blocks = group_ref.shape[0]

    @pl.when(step < early)
    def _():
        value = product(embed_ref[...], trunk_ref[...]) + trunk_bias_ref[...]
        at = pl.multiple_of(step * wide, wide)
        hidden_ref[:, pl.ds(at, wide)] = jax.nn.silu(value).astype(BF16)

    @pl.when(step >= early)
    def _():
        block = step - early
        out = product(hidden_ref[...], weight_ref[...]) + bias_ref[...]
        col = iota((256, 256), 0)
        target = ((col >> 3) & 1) * 128 + ((block + col) & 7) * 16 + (col >> 4)
        perm = one_where(iota((256, 256), 1) == target)
        group_ref[block] = product(out.astype(BF16), perm).astype(BF16)

    @pl.when(step == early + blocks - 1)
    def _():
        group = lane_group(16)
        masks = [group == jnp.asarray(place, BF16) for place in range(8)]

        def mix(index, carry):
            span = pl.ds(pl.multiple_of(index * 16, 16), 16)
            for side in range(2):
                lanes = slice(side * LANES, side * LANES + LANES)
                tiles = [group_ref[block, span, lanes] for block in range(8)]
                for turn in range(8):
                    mixed = tiles[0]
                    for block in range(1, 8):
                        mixed = jnp.where(masks[(block + turn) % 8], tiles[block], mixed)
                    out_ref[side * 8 + turn, span] = mixed
            return carry

        lax.fori_loop(0, entries // 16, mix, 0, unroll=4)


def table_factors(embed, trunk, trunk_bias, head_weight, bias):
    entries, width = embed.shape
    hid, cols = head_weight.shape
    early, blocks = hid // 512, cols // 256
    first = lambda i: (0, jnp.minimum(i, early - 1))
    then = lambda i: (0, jnp.maximum(i - early, 0))
    return pl.pallas_call(
        table_kernel,
        grid=(early + blocks,),
        in_specs=[
            pl.BlockSpec(embed.shape, lambda i: (0, 0)),
            pl.BlockSpec((width, 512), first),
            pl.BlockSpec((1, 512), first),
            pl.BlockSpec((hid, 256), then),
            pl.BlockSpec((1, 256), then),
        ],
        out_specs=pl.BlockSpec((16, entries, LANES), lambda i: (0, 0, 0)),
        out_shape=jax.ShapeDtypeStruct((16, entries, LANES), BF16),
        scratch_shapes=[
            pltpu.VMEM((entries, hid), BF16),
            pltpu.VMEM((blocks, entries, 256), BF16),
        ],
        cost_estimate=cost(2 * entries * hid * (width + cols), 18 << 20),
        name="table",
    )(embed, trunk, trunk_bias, head_weight, bias)


def pick_kernel(id_ref, table_ref, out_ref, hot_ref):
    step = pl.program_id(0)
    tasks, rows = id_ref.shape
    dests, entries, _ = table_ref.shape

    @pl.when(step == 0)
    def _():
        lane = iota((rows, LANES), 1).astype(F32)
        for task in range(tasks):
            ids = jnp.broadcast_to(id_ref[task : task + 1, :].astype(F32), (LANES, rows)).T
            for at in range(0, entries, LANES):
                hot_ref[task * rows : (task + 1) * rows, at : at + LANES] = one_where(
                    ids == lane + float(at)
                )

    for at in range(0, dests, 2):
        pair = jnp.concatenate([table_ref[at], table_ref[at + 1]], axis=1)
        picked = product(hot_ref[...], pair)
        for side in range(2):
            turn = (dests * step + at + side) & 7
            piece = picked[:, side * LANES : side * LANES + LANES]
            piece = pltpu.roll(piece, (8 - turn) * 16, 1).astype(BF16)
            out_ref[:, at + side] = piece.reshape(tasks, rows, LANES)


def picked_rows(ids, factors):
    tasks, rows = ids.shape
    dests, entries, _ = factors.shape
    span = 4
    return pl.pallas_call(
        pick_kernel,
        grid=(dests // span,),
        in_specs=[
            pl.BlockSpec(ids.shape, lambda i: (0, 0)),
            pl.BlockSpec((span, entries, LANES), lambda i: (i, 0, 0)),
        ],
        out_specs=pl.BlockSpec((tasks, span, rows, LANES), lambda i: (0, i, 0, 0)),
        out_shape=jax.ShapeDtypeStruct((tasks, dests, rows, LANES), BF16),
        scratch_shapes=[pltpu.VMEM((tasks * rows, entries), BF16)],
        cost_estimate=cost(2 * tasks * rows * entries * dests * LANES, 8 << 20),
        name="pick",
    )(ids, factors)


def sort_kernel(all_ref, row_ref, in_ref, out_ref, low_ref, part_ref, name_ref, rank_ref, slot_ref):
    step = pl.program_id(0)
    tokens = all_ref.shape[1]
    width, tile = out_ref.shape
    count = 128
    per_row = tokens // count

    @pl.when(step == 0)
    def _():
        before = one_where(iota((256, 256), 0) < iota((256, 256), 1))
        carry = jnp.zeros((count, 1), F32)
        for at in range(0, tokens, 256):
            rows = all_ref[:, at : at + 256]
            hot = jnp.where(iota((count, 256), 0) == rows, 1.0, 0.0)
            seen = product(hot.astype(BF16), before) + carry
            rank = jnp.sum(hot * seen, axis=0, keepdims=True).astype(jnp.int32)
            carry = carry + jnp.sum(hot, axis=1, keepdims=True)
            slot = rows * per_row + rank
            slot_ref[:, at : at + 256] = slot
            rank_ref[at // 256] = slot

    total = jnp.zeros((tile, width), F32)
    for at in range(0, tokens, 1024):
        place = iota((tile, 1024), 0) + step * tile
        hot = one_where(place == slot_ref[:, at : at + 1024])
        total = total + product(hot, in_ref[at : at + 1024, :])
    out_ref[...] = total.T.astype(BF16)

    for at in range(0, tile, 256):
        slot = rank_ref[step * (tile // 256) + at // 256]
        slot = jnp.broadcast_to(slot.astype(F32), (LANES, 256)).T.astype(jnp.int32)
        span = slice(at, at + 256)
        lane = iota((256, LANES), 1)
        low_ref[span, :LANES] = one_where((slot & 255) == lane)
        low_ref[span, LANES:] = one_where((slot & 255) == lane + LANES)
        part_ref[span, :] = (slot >> 8).astype(F32).astype(BF16)
        name_ref[span, :] = (slot // per_row).astype(F32).astype(BF16)


def sorted_tokens(local_row, inputs):
    tokens, width = inputs.shape
    tile = 512
    wide = lambda lanes: jax.ShapeDtypeStruct((tokens, lanes), BF16)
    return pl.pallas_call(
        sort_kernel,
        grid=(tokens // tile,),
        in_specs=[
            pl.BlockSpec((1, tokens), lambda i: (0, 0)),
            pl.BlockSpec((1, tile), lambda i: (0, i)),
            pl.BlockSpec((tokens, width), lambda i: (0, 0)),
        ],
        out_specs=[
            pl.BlockSpec((width, tile), lambda i: (0, i)),
            pl.BlockSpec((tile, 256), lambda i: (i, 0)),
            pl.BlockSpec((tile, LANES), lambda i: (i, 0)),
            pl.BlockSpec((tile, LANES), lambda i: (i, 0)),
        ],
        out_shape=[jax.ShapeDtypeStruct((width, tokens), BF16), wide(256), wide(LANES), wide(LANES)],
        scratch_shapes=[
            pltpu.VMEM((tokens // 256, 1, 256), jnp.int32),
            pltpu.VMEM((1, tokens), jnp.int32),
        ],
        cost_estimate=cost(2 * tokens * tokens * width, 16 << 20),
        name="sort",
    )(local_row, local_row, inputs)


def entry_kernel(in_ref, block_ref, out_ref):
    rows = block_ref.shape[3]
    part = 16
    slots = in_ref.shape[1] * part // rows
    match = iota((part, slots), 0) == iota((part, slots), 1) // (slots // part)
    for at in range(0, rows, part):
        span = slice(at, at + part)
        factor = jnp.concatenate(
            [block_ref[0, :, q, span].reshape(RANK * part, LANES) for q in range(4)], axis=1
        )
        first = at // part * slots
        scores = product(factor, in_ref[:, first : first + slots])
        scores = jnp.where(match[None], scores.reshape(RANK, part, slots), 0.0)
        coef = jnp.sum(scores, axis=1).astype(out_ref.dtype)
        for piece in range(0, slots, 256):
            out_ref[(first + piece) // 256] = coef[:, piece : piece + 256]


def rank_parts(inputs, blocks):
    width, tokens = inputs.shape
    rows = blocks.shape[3]
    steps = 2
    return pl.pallas_call(
        entry_kernel,
        grid=(steps,),
        in_specs=[
            pl.BlockSpec((width, tokens // steps), lambda i: (0, i)),
            pl.BlockSpec((1, RANK, 4, rows // steps, LANES), lambda i: (0, 0, 0, i, 0)),
        ],
        out_specs=pl.BlockSpec((tokens // steps // 256, RANK, 256), lambda i: (i, 0, 0)),
        out_shape=jax.ShapeDtypeStruct((tokens // 256, RANK, 256), BF16),
        name="entry",
    )(inputs, blocks)


def order_kernel(block_ref, out_ref):
    out_at = iota((256, 256), 0)
    perm = one_where(iota((256, 256), 1) == (out_at & 15) * 16 + (out_at >> 4))
    for at in range(0, block_ref.shape[3], 16):
        piece = jnp.concatenate(
            [block_ref[0, :, q, at : at + 16].reshape(RANK * 16, LANES) for q in range(4)],
            axis=1,
        )
        out_ref[at * RANK : at * RANK + 256] = product(perm, piece).astype(BF16)


def ordered_exit(blocks):
    rows = blocks.shape[3]
    part = rows // 2
    return pl.pallas_call(
        order_kernel,
        grid=(rows // part,),
        in_specs=[pl.BlockSpec((1, RANK, 4, part, LANES), lambda i: (1, 0, 0, i, 0))],
        out_specs=pl.BlockSpec((part * RANK, 4 * LANES), lambda i: (i, 0)),
        out_shape=jax.ShapeDtypeStruct((rows * RANK, 4 * LANES), BF16),
        name="order",
    )(blocks)


def exit_kernel(coef_ref, low_ref, part_ref, name_ref, base_ref, factor_ref, out_ref):
    tile = base_ref.shape[0]
    depth = factor_ref.shape[0]
    group = lane_group(tile)
    zero = jnp.zeros((tile, LANES), F32)
    values = product(low_ref[...], coef_ref[...], 1, 1)
    part = part_ref[...].astype(F32)
    group32 = group.astype(F32)
    mine = jnp.where(part == group32, values[:, :LANES], zero)
    mine = mine + jnp.where(part == group32 + 8.0, values[:, LANES:], zero)
    fold = one_where((iota((LANES, LANES), 0) & 15) == (iota((LANES, LANES), 1) & 15))
    coef = product(mine.astype(BF16), fold).astype(BF16)
    name = name_ref[...]
    spread = jnp.concatenate(
        [
            jnp.where(name == group + jnp.asarray(at, BF16), coef, jnp.zeros_like(coef))
            for at in range(0, depth // RANK, 8)
        ],
        axis=1,
    )
    update = product(spread, factor_ref[...])
    base = base_ref[...].astype(F32)
    out_ref[...] = (base + update * (1.0 / math.sqrt(RANK))).astype(BF16)


def apply_update(coefs, low, part, name, base, factors):
    tokens, width = base.shape
    tile = 1024
    return pl.pallas_call(
        exit_kernel,
        grid=(tokens // tile,),
        in_specs=[
            pl.BlockSpec(coefs.shape, lambda i: (0, 0)),
            pl.BlockSpec((tile, 256), lambda i: (i, 0)),
            pl.BlockSpec((tile, LANES), lambda i: (i, 0)),
            pl.BlockSpec((tile, LANES), lambda i: (i, 0)),
            pl.BlockSpec((tile, width), lambda i: (i, 0)),
            pl.BlockSpec(factors.shape, lambda i: (0, 0)),
        ],
        out_specs=pl.BlockSpec((tile, width), lambda i: (i, 0)),
        out_shape=jax.ShapeDtypeStruct((tokens, width), BF16),
        name="exit",
    )(coefs, low, part, name, base, factors)


def to_all(shard, axis):
    length = lax.axis_size(axis)
    return lax.all_to_all(
        jnp.broadcast_to(shard[None], (length, *shard.shape)), axis, 0, 0, tiled=True
    )


def on_device(
    task_ids,
    embed_table,
    trunk_weight,
    trunk_bias,
    head_weight,
    head_bias,
    token_row,
    inputs,
    frozen,
):
    tasks = lax.axis_size("task")
    width = lax.axis_size("width")
    rows_dev = task_ids.shape[0]
    me = lax.axis_index("task")
    ids = to_all(task_ids, "task").reshape(tasks, rows_dev)
    factors = table_factors(
        embed_table,
        trunk_weight,
        trunk_bias.reshape(1, -1),
        head_weight,
        head_bias.reshape(1, -1),
    )
    blocks = picked_rows(ids, factors)
    moved = lax.all_to_all(
        blocks.reshape(tasks * width, rows_dev, LANES), BOTH, 0, 0, tiled=True
    ).reshape(2, RANK, 4, rows_dev, LANES)

    local_row = (token_row - me * rows_dev).reshape(1, -1)
    in_order, low, part, name = sorted_tokens(local_row, inputs)
    parts = rank_parts(in_order, moved)
    pieces = lax.all_to_all(parts, "width", 0, 0, tiled=True).astype(F32)
    coef = (pieces.sum(axis=0) * (1.0 / math.sqrt(WIDTH))).astype(BF16)
    coefs = to_all(coef, "width").reshape(width * RANK, -1)
    return apply_update(coefs, low, part, name, frozen, ordered_exit(moved))


def solution(mesh):
    return jax.shard_map(
        on_device,
        mesh=mesh,
        in_specs=(
            P("task"),
            P(),
            P(),
            P(),
            P(None, BOTH),
            P(BOTH),
            P("task"),
            P("task", "width"),
            P("task", "width"),
        ),
        out_specs=P("task", "width"),
        check_vma=False,
    )
```

time: 157 us -> 147 us (0.936)
  matrix products: 9.92 us -> 0 us
  Pallas kernels: 83.5 us -> 78.9 us
  starting transfers between devices: 19 us -> 23 us
  waiting for transfers between devices: 28.2 us -> 30.4 us
    dot_general x2 -> x0, matrix products: 9.92 us -> none  [on_device(): jnp.dot(embed_table, trunk_weight[:, cut], preferred_element_type=F32)]
    ppermute x3 -> x0, starting transfers between devices: 8.49 us -> none  [gathered(): moved = lax.ppermute(held, axis, [(at, at ^ step) for at in range(length)])]
    all_to_all x1 -> x2, starting transfers between devices: 4.06 us -> 12.2 us  [to_all(): lax.all_to_all(jnp.broadcast_to(shard[None], (length, *shard.shape)), axi...]
    pallas_call x4, Pallas kernels: 43.9 us -> 39.4 us  [the longest x1 23.7 us: table_factors(): pl.pallas_call(table_kernel, grid=(early + blocks,), in_specs=[pl.BlockSp...]
    all_to_all x1, starting transfers between devices: 6.41 us -> 10.8 us  [on_device(): lax.all_to_all(blocks.reshape(tasks * width, rows_dev, LANES), BOTH, 0, 0...]
    all_to_all x1 -> x2, waiting for transfers between devices: 0.01 us -> 2.98 us  [to_all(): lax.all_to_all(jnp.broadcast_to(shard[None], (length, *shard.shape)), axi...]
  transfers between devices with their start and end apart: 5 -> 3, of which waited for: 1 -> 2; matrix products, arithmetic and copies ran while one was open for 7% -> 0% of each run, Pallas kernels for 32% -> 35%
where the time goes in v2:
time: 147 us; the launch traced here: 146 us
  Pallas kernels  78.9 us (54%)
  waiting for transfers between devices  30.4 us (21%)
  starting transfers between devices  23 us (16%)
  blocking collectives  10.4 us (7%)
  local copies, waits for them, and re-layouts  3.15 us (2%)
    all_to_all x1, waiting for transfers between devices, on_device(): lax.all_to_all(blocks.reshape(tasks * width, rows_dev, LANES), BOTH, 0, 0...  27.4 us
    pallas_call x1, Pallas kernels, sorted_tokens(): pl.pallas_call(sort_kernel, grid=(tokens // tile,), in_specs=[pl.BlockSpe...  24.6 us
    pallas_call x1, Pallas kernels, table_factors(): pl.pallas_call(table_kernel, grid=(early + blocks,), in_specs=[pl.BlockSp...  23.7 us
    pallas_call x1, Pallas kernels, apply_update(): pl.pallas_call(exit_kernel, grid=(tokens // tile,), in_specs=[pl.BlockSpe...  14.9 us
    all_to_all x2, starting transfers between devices, to_all(): lax.all_to_all(jnp.broadcast_to(shard[None], (length, *shard.shape)), axi...  12.2 us
    all_to_all x1, starting transfers between devices, on_device(): lax.all_to_all(blocks.reshape(tasks * width, rows_dev, LANES), BOTH, 0, 0...  10.8 us
    all_to_all x1, blocking collectives, on_device(): pieces = lax.all_to_all(parts, 'width', 0, 0, tiled=True).astype(F32)  10.4 us
    pallas_call x1, Pallas kernels, picked_rows(): pl.pallas_call(pick_kernel, grid=(dests // span,), in_specs=[pl.BlockSpec...  8.36 us
  transfers between devices with their start and end apart: 3, of which 2 were waited for; matrix products, arithmetic and copies ran while one was open for 0% of the time, Pallas kernels for 35%

profile of v2, /device:TPU:1, one launch (start us, length us, event | category | flops | bytes accessed | tf_op | source)
XLA Modules:
  0.0 146.4 jit_solution(5261733868752318700)
XLA Ops:
  0.0 1.2 broadcast_in_dim.4
  1.2 8.3 %all-to-all-start = ((s32[8,1,128]{2,1,0:T(1,128)}), s32[8,1,128]{2,1,0:T(1,128)S(1)}, u32[]{:S(2)}, u32[]{:S(2)}) async-start(s32[8,1,128]{2,1,0:T(1,128)} %broadcast_in_dim.4), calls=%async_computation | async-start | bytes 8192 | tf_op jit(solution)/shard_map/all_to_all | solution.py:327
  9.6 23.7 %table.1.table_ref = bf16[16,1024,128]{2,1,0:T(8,128)(2,1)} custom-call(bf16[1024,1024]{1,0:T(8,128)(2,1)} %embed_ref.1, bf16[1024,2048]{1,0:T(8,128)(2,1)} %trunk_ref.1, f32[1,2048]{1,0:T(1,128)} %bitcast.12, bf16[2048,2048]{1,0:T(8,128)(2,1)} %weight_ref.1, f32[1,2048]{1,0:T(1,128)} %bitcast.13), custom_call_target="tpu_custom_call" | custom-call | flops 12884901888 | bytes 18874368 | tf_op jit(solution)/shard_map/table/pallas_call | solution.py:89
  33.3 0.0 all-to-all-done
  33.3 0.0 copy-start.2
  33.3 0.6 copy-done.2
  33.9 8.4 %pick.1 = bf16[8,16,128,128]{3,2,1,0:T(8,128)(2,1)} custom-call(s32[8,128]{1,0:T(8,128)} %bitcast.11, bf16[16,1024,128]{2,1,0:T(8,128)(2,1)} %table.1.table_ref), custom_call_target="tpu_custom_call" | custom-call | flops 4294967296 | bytes 8388608 | tf_op jit(solution)/shard_map/pick/pallas_call | solution.py:139
  42.2 0.0 copy-start.1
  42.2 10.8 %all-to-all-start.1 = ((bf16[128,128,128]{2,1,0:T(8,128)(2,1)}), bf16[128,128,128]{2,1,0:T(8,128)(2,1)}, u32[]{:S(2)}, u32[]{:S(2)}) async-start(bf16[128,128,128]{2,1,0:T(8,128)(2,1)} %bitcast.7), calls=%async_computation.1 | async-start | bytes 8388608 | tf_op jit(solution)/shard_map/all_to_all | solution.py:356
  53.0 0.0 copy-done.1
  53.0 0.6 broadcast_subtract_fusion
  53.6 24.6 %sort.1 = (bf16[512,4096]{1,0:T(8,128)(2,1)}, bf16[4096,256]{1,0:T(8,128)(2,1)}, bf16[4096,128]{1,0:T(8,128)(2,1)}, bf16[4096,128]{1,0:T(8,128)(2,1)}) custom-call(s32[1,4096]{1,0:T(1,128)} %bitcast.9, s32[1,4096]{1,0:T(1,128)} %bitcast.10, bf16[4096,512]{1,0:T(8,128)(2,1)} %in_ref.1), custom_call_target="tpu_custom_call" | custom-call | flops 17179869184 | bytes 16777216 | tf_op jit(solution)/shard_map/sort/pallas_call | solution.py:197
  78.2 27.4 %all-to-all-done.1 = bf16[128,128,128]{2,1,0:T(8,128)(2,1)} async-done(((bf16[128,128,128]{2,1,0:T(8,128)(2,1)}), bf16[128,128,128]{2,1,0:T(8,128)(2,1)}, u32[]{:S(2)}, u32[]{:S(2)}) %all-to-all-start.1) | async-done | bytes 4194336 | tf_op jit(solution)/shard_map/all_to_all | solution.py:356
  105.6 4.2 %entry.1 = bf16[16,16,256]{2,1,0:T(8,128)(2,1)} custom-call(bf16[512,4096]{1,0:T(8,128)(2,1)} %get-tuple-element.9.in_ref, bf16[2,16,4,128,128]{4,3,2,1,0:T(8,128)(2,1)} %bitcast.5.block_ref), custom_call_target="tpu_custom_call" | custom-call | tf_op jit(solution)/shard_map/entry/pallas_call | solution.py:243
  109.8 10.4 %all_to_all.23 = bf16[16,16,256]{2,1,0:T(8,128)(2,1)S(1)} all-to-all(bf16[16,16,256]{2,1,0:T(8,128)(2,1)} %entry.1), channel_id=1, replica_groups=mesh['task'=8,'width'=16] {'width'}, dimensions={0} | all-to-all | bytes 262144 | tf_op jit(solution)/shard_map/all_to_all | solution.py:363
  120.2 0.7 broadcast_in_dim.5
  120.9 3.8 %all-to-all-start.3 = ((bf16[16,16,256]{2,1,0:T(8,128)(2,1)}), bf16[16,16,256]{2,1,0:T(8,128)(2,1)S(1)}, u32[]{:S(2)}, u32[]{:S(2)}) async-start(bf16[16,16,256]{2,1,0:T(8,128)(2,1)} %broadcast_in_dim.5), calls=%async_computation.3 | async-start | bytes 262144 | tf_op jit(solution)/shard_map/all_to_all | solution.py:327
  124.7 3.2 %order.1.factor_ref = bf16[2048,512]{1,0:T(8,128)(2,1)} custom-call(bf16[2,16,4,128,128]{4,3,2,1,0:T(8,128)(2,1)} %bitcast.5.block_ref), custom_call_target="tpu_custom_call" | custom-call | tf_op jit(solution)/shard_map/order/pallas_call | solution.py:270
  127.9 3.0 %all-to-all-done.3 = bf16[16,16,256]{2,1,0:T(8,128)(2,1)S(1)} async-done(((bf16[16,16,256]{2,1,0:T(8,128)(2,1)}), bf16[16,16,256]{2,1,0:T(8,128)(2,1)S(1)}, u32[]{:S(2)}, u32[]{:S(2)}) %all-to-all-start.3) | async-done | bytes 131104 | tf_op jit(solution)/shard_map/all_to_all | solution.py:327
  130.9 0.0 copy-start
  130.9 0.6 copy-done
  131.5 14.9 %exit.1 = bf16[4096,512]{1,0:T(8,128)(2,1)} custom-call(bf16[256,256]{1,0:T(8,128)(2,1)} %bitcast.8, bf16[4096,256]{1,0:T(8,128)(2,1)} %get-tuple-element.10.low_ref, bf16[4096,128]{1,0:T(8,128)(2,1)} %get-tuple-element.11.part_ref, bf16[4096,128]{1,0:T(8,128)(2,1)} %get-tuple-element.12.name_ref, bf16[4096,512]{1,0:T(8,128)(2,1)} %base_ref.1, ...), custom_call_target="tpu_custom_call" | custom-call | tf_op jit(solution)/shard_map/exit/pallas_call | solution.py:308
  (2 shorter events, 0.0 us)
Async XLA Ops:
  1.2 32.0 %all-to-all-start = ((s32[8,1,128]{2,1,0:T(1,128)}), s32[8,1,128]{2,1,0:T(1,128)S(1)}, u32[]{:S(2)}, u32[]{:S(2)}) async-start(s32[8,1,128]{2,1,0:T(1,128)} %broadcast_in_dim.4), calls=%async_computation | async-start | bytes 8192 | tf_op jit(solution)/shard_map/all_to_all | solution.py:327
  33.3 0.6 copy-start.2
  42.2 10.8 %copy-start.1 = (s32[4096]{0:T(1024)S(1)}, s32[4096]{0:T(1024)}, u32[]{:S(2)}) copy-start(s32[4096]{0:T(1024)} %param.15) | copy-start | bytes 49156
  42.2 63.4 %all-to-all-start.1 = ((bf16[128,128,128]{2,1,0:T(8,128)(2,1)}), bf16[128,128,128]{2,1,0:T(8,128)(2,1)}, u32[]{:S(2)}, u32[]{:S(2)}) async-start(bf16[128,128,128]{2,1,0:T(8,128)(2,1)} %bitcast.7), calls=%async_computation.1 | async-start | bytes 8388608 | tf_op jit(solution)/shard_map/all_to_all | solution.py:356
  120.9 10.0 %all-to-all-start.3 = ((bf16[16,16,256]{2,1,0:T(8,128)(2,1)}), bf16[16,16,256]{2,1,0:T(8,128)(2,1)S(1)}, u32[]{:S(2)}, u32[]{:S(2)}) async-start(bf16[16,16,256]{2,1,0:T(8,128)(2,1)} %broadcast_in_dim.5), calls=%async_computation.3 | async-start | bytes 262144 | tf_op jit(solution)/shard_map/all_to_all | solution.py:327
  130.9 0.7 copy-start

commit v3 on v2

--- a/solution.py
+++ b/solution.py
@@ -13,6 +13,8 @@
 BOTH = ("task", "width")
 BF16 = jnp.bfloat16
 F32 = jnp.float32
+HELD = pl.BlockSpec(memory_space=pltpu.VMEM)
+ROOM = pltpu.CompilerParams(vmem_limit_bytes=40 << 20)
 
 
 def product(a, b, a_dim=1, b_dim=0):
@@ -36,20 +38,18 @@
 
 
 def table_kernel(
-    embed_ref, trunk_ref, trunk_bias_ref, weight_ref, bias_ref, out_ref, hidden_ref, group_ref
+    embed_ref, trunk_ref, trunk_bias_ref, weight_ref, bias_ref, out_ref, hidden_ref
 ):
     step = pl.program_id(0)
-    entries = embed_ref.shape[0]
     hid = hidden_ref.shape[1]
-    wide = trunk_ref.shape[1]
+    wide = 512
     early = hid // wide
-    blocks = group_ref.shape[0]
 
     @pl.when(step < early)
     def _():
+        span = pl.ds(pl.multiple_of(step * wide, wide), wide)
         value = product(embed_ref[...], trunk_ref[...]) + trunk_bias_ref[...]
-        at = pl.multiple_of(step * wide, wide)
-        hidden_ref[:, pl.ds(at, wide)] = jax.nn.silu(value).astype(BF16)
+        hidden_ref[:, span] = jax.nn.silu(value).astype(BF16)
 
     @pl.when(step >= early)
     def _():
@@ -58,26 +58,7 @@
         col = iota((256, 256), 0)
         target = ((col >> 3) & 1) * 128 + ((block + col) & 7) * 16 + (col >> 4)
         perm = one_where(iota((256, 256), 1) == target)
-        group_ref[block] = product(out.astype(BF16), perm).astype(BF16)
-
-    @pl.when(step == early + blocks - 1)
-    def _():
-        group = lane_group(16)
-        masks = [group == jnp.asarray(place, BF16) for place in range(8)]
-
-        def mix(index, carry):
-            span = pl.ds(pl.multiple_of(index * 16, 16), 16)
-            for side in range(2):
-                lanes = slice(side * LANES, side * LANES + LANES)
-                tiles = [group_ref[block, span, lanes] for block in range(8)]
-                for turn in range(8):
-                    mixed = tiles[0]
-                    for block in range(1, 8):
-                        mixed = jnp.where(masks[(block + turn) % 8], tiles[block], mixed)
-                    out_ref[side * 8 + turn, span] = mixed
-            return carry
-
-        lax.fori_loop(0, entries // 16, mix, 0, unroll=4)
+        out_ref[0] = product(out.astype(BF16), perm).astype(BF16)
 
 
 def table_factors(embed, trunk, trunk_bias, head_weight, bias):
@@ -96,23 +77,22 @@
             pl.BlockSpec((hid, 256), then),
             pl.BlockSpec((1, 256), then),
         ],
-        out_specs=pl.BlockSpec((16, entries, LANES), lambda i: (0, 0, 0)),
-        out_shape=jax.ShapeDtypeStruct((16, entries, LANES), BF16),
-        scratch_shapes=[
-            pltpu.VMEM((entries, hid), BF16),
-            pltpu.VMEM((blocks, entries, 256), BF16),
-        ],
+        out_specs=pl.BlockSpec(
+            (1, entries, 256), lambda i: (jnp.maximum(i - early, 0), 0, 0)
+        ),
+        out_shape=jax.ShapeDtypeStruct((blocks, entries, 256), BF16),
+        scratch_shapes=[pltpu.VMEM((entries, hid), BF16)],
         cost_estimate=cost(2 * entries * hid * (width + cols), 18 << 20),
         name="table",
     )(embed, trunk, trunk_bias, head_weight, bias)
 
 
-def pick_kernel(id_ref, table_ref, out_ref, hot_ref):
-    step = pl.program_id(0)
+def pick_kernel(id_ref, table_ref, out_ref, hot_ref, mixed_ref):
     tasks, rows = id_ref.shape
-    dests, entries, _ = table_ref.shape
-
-    @pl.when(step == 0)
+    blocks, entries, _ = table_ref.shape
+    half = pl.program_id(0)
+
+    @pl.when(half == 0)
     def _():
         lane = iota((rows, LANES), 1).astype(F32)
         for task in range(tasks):
@@ -122,31 +102,43 @@
                     ids == lane + float(at)
                 )
 
-    for at in range(0, dests, 2):
-        pair = jnp.concatenate([table_ref[at], table_ref[at + 1]], axis=1)
-        picked = product(hot_ref[...], pair)
+    group = lane_group(entries)
+
+    def mix(first):
+        for turn in (first, first + 1):
+            mixed = table_ref[0]
+            for block in range(1, blocks):
+                place = jnp.asarray((block + turn) % 8, BF16)
+                mixed = jnp.where(group == place, table_ref[block], mixed)
+            mixed_ref[:, turn * LANES : (turn + 1) * LANES] = mixed
+
+    mix(0)
+    for first in range(0, 8, 2):
+        if first + 2 < 8:
+            mix(first + 2)
+        picked = product(hot_ref[...], mixed_ref[:, first * LANES : (first + 2) * LANES])
         for side in range(2):
-            turn = (dests * step + at + side) & 7
+            turn = first + side
             piece = picked[:, side * LANES : side * LANES + LANES]
-            piece = pltpu.roll(piece, (8 - turn) * 16, 1).astype(BF16)
-            out_ref[:, at + side] = piece.reshape(tasks, rows, LANES)
+            if turn:
+                piece = pltpu.roll(piece, LANES - 16 * turn, 1)
+            out_ref[:, turn] = piece.astype(BF16).reshape(tasks, rows, LANES)
 
 
 def picked_rows(ids, factors):
     tasks, rows = ids.shape
-    dests, entries, _ = factors.shape
-    span = 4
+    blocks, entries, _ = factors.shape
     return pl.pallas_call(
         pick_kernel,
-        grid=(dests // span,),
-        in_specs=[
-            pl.BlockSpec(ids.shape, lambda i: (0, 0)),
-            pl.BlockSpec((span, entries, LANES), lambda i: (i, 0, 0)),
-        ],
-        out_specs=pl.BlockSpec((tasks, span, rows, LANES), lambda i: (0, i, 0, 0)),
-        out_shape=jax.ShapeDtypeStruct((tasks, dests, rows, LANES), BF16),
-        scratch_shapes=[pltpu.VMEM((tasks * rows, entries), BF16)],
-        cost_estimate=cost(2 * tasks * rows * entries * dests * LANES, 8 << 20),
+        grid=(2,),
+        in_specs=[HELD, pl.BlockSpec((blocks, entries, LANES), lambda i: (0, 0, i))],
+        out_specs=pl.BlockSpec((tasks, 8, rows, LANES), lambda i: (0, i, 0, 0)),
+        out_shape=jax.ShapeDtypeStruct((tasks, 16, rows, LANES), BF16),
+        scratch_shapes=[
+            pltpu.VMEM((tasks * rows, entries), BF16),
+            pltpu.VMEM((entries, 8 * LANES), BF16),
+        ],
+        cost_estimate=cost(2 * tasks * rows * entries * 16 * LANES, 8 << 20),
         name="pick",
     )(ids, factors)
 
@@ -273,6 +265,7 @@
         in_specs=[pl.BlockSpec((1, RANK, 4, part, LANES), lambda i: (1, 0, 0, i, 0))],
         out_specs=pl.BlockSpec((part * RANK, 4 * LANES), lambda i: (i, 0)),
         out_shape=jax.ShapeDtypeStruct((rows * RANK, 4 * LANES), BF16),
+        compiler_params=ROOM,
         name="order",
     )(blocks)
 
@@ -282,7 +275,7 @@
     depth = factor_ref.shape[0]
     group = lane_group(tile)
     zero = jnp.zeros((tile, LANES), F32)
-    values = product(low_ref[...], coef_ref[...], 1, 1)
+    values = product(low_ref[...], coef_ref[...].reshape(256, 256), 1, 1)
     part = part_ref[...].astype(F32)
     group32 = group.astype(F32)
     mine = jnp.where(part == group32, values[:, :LANES], zero)
@@ -305,19 +298,24 @@
 def apply_update(coefs, low, part, name, base, factors):
     tokens, width = base.shape
     tile = 1024
+    low, part, name, base = (
+        pltpu.with_memory_space_constraint(array, pltpu.MemorySpace.HBM)
+        for array in (low, part, name, base)
+    )
     return pl.pallas_call(
         exit_kernel,
         grid=(tokens // tile,),
         in_specs=[
-            pl.BlockSpec(coefs.shape, lambda i: (0, 0)),
+            HELD,
             pl.BlockSpec((tile, 256), lambda i: (i, 0)),
             pl.BlockSpec((tile, LANES), lambda i: (i, 0)),
             pl.BlockSpec((tile, LANES), lambda i: (i, 0)),
             pl.BlockSpec((tile, width), lambda i: (i, 0)),
-            pl.BlockSpec(factors.shape, lambda i: (0, 0)),
+            HELD,
         ],
         out_specs=pl.BlockSpec((tile, width), lambda i: (i, 0)),
         out_shape=jax.ShapeDtypeStruct((tokens, width), BF16),
+        compiler_params=ROOM,
         name="exit",
     )(coefs, low, part, name, base, factors)
 
@@ -362,7 +360,7 @@
     parts = rank_parts(in_order, moved)
     pieces = lax.all_to_all(parts, "width", 0, 0, tiled=True).astype(F32)
     coef = (pieces.sum(axis=0) * (1.0 / math.sqrt(WIDTH))).astype(BF16)
-    coefs = to_all(coef, "width").reshape(width * RANK, -1)
+    coefs = to_all(coef, "width")
     return apply_update(coefs, low, part, name, frozen, ordered_exit(moved))
 
 

time: 147 us -> 144 us (0.980)
  Pallas kernels: 78.9 us -> 75.3 us
    pallas_call x1, Pallas kernels: 23.7 us -> 21.4 us  [table_factors(): pl.pallas_call(table_kernel, grid=(early + blocks,), in_specs=[pl.BlockSp...]
  transfers between devices with their start and end apart: 3 -> 3, of which waited for: 2 -> 2; matrix products, arithmetic and copies ran while one was open for 0% -> 0% of each run, Pallas kernels for 35% -> 34%
where the time goes in v3:
time: 144 us; the launch traced here: 143 us
  Pallas kernels  75.3 us (52%)
  waiting for transfers between devices  31.4 us (22%)
  starting transfers between devices  23 us (16%)
  blocking collectives  10.4 us (7%)
  local copies, waits for them, and re-layouts  2.51 us (2%)
    all_to_all x1, waiting for transfers between devices, on_device(): lax.all_to_all(blocks.reshape(tasks * width, rows_dev, LANES), BOTH, 0, 0...  27.4 us
    pallas_call x1, Pallas kernels, sorted_tokens(): pl.pallas_call(sort_kernel, grid=(tokens // tile,), in_specs=[pl.BlockSpe...  24.6 us
    pallas_call x1, Pallas kernels, table_factors(): pl.pallas_call(table_kernel, grid=(early + blocks,), in_specs=[pl.BlockSp...  21.4 us
    pallas_call x1, Pallas kernels, apply_update(): pl.pallas_call(exit_kernel, grid=(tokens // tile,), in_specs=[HELD, pl.Bl...  13.9 us
    all_to_all x2, starting transfers between devices, to_all(): lax.all_to_all(jnp.broadcast_to(shard[None], (length, *shard.shape)), axi...  12.2 us
    all_to_all x1, starting transfers between devices, on_device(): lax.all_to_all(blocks.reshape(tasks * width, rows_dev, LANES), BOTH, 0, 0...  10.8 us
    all_to_all x1, blocking collectives, on_device(): pieces = lax.all_to_all(parts, 'width', 0, 0, tiled=True).astype(F32)  10.4 us
    pallas_call x1, Pallas kernels, picked_rows(): pl.pallas_call(pick_kernel, grid=(2,), in_specs=[HELD, pl.BlockSpec((bloc...  9.01 us
  transfers between devices with their start and end apart: 3, of which 2 were waited for; matrix products, arithmetic and copies ran while one was open for 0% of the time, Pallas kernels for 34%

profile of v3, /device:TPU:1, one launch (start us, length us, event | category | flops | bytes accessed | tf_op | source)
XLA Modules:
  0.0 143.2 jit_solution(2325858746232049827)
XLA Ops:
  0.0 1.2 broadcast_in_dim.4
  1.3 8.3 %all-to-all-start = ((s32[8,1,128]{2,1,0:T(1,128)}), s32[8,1,128]{2,1,0:T(1,128)S(1)}, u32[]{:S(2)}, u32[]{:S(2)}) async-start(s32[8,1,128]{2,1,0:T(1,128)} %broadcast_in_dim.4), calls=%async_computation | async-start | bytes 8192 | tf_op jit(solution)/shard_map/all_to_all | solution.py:325
  9.6 21.4 %table.1.table_ref = bf16[8,1024,256]{2,1,0:T(8,128)(2,1)} custom-call(bf16[1024,1024]{1,0:T(8,128)(2,1)} %embed_ref.1, bf16[1024,2048]{1,0:T(8,128)(2,1)} %trunk_ref.1, f32[1,2048]{1,0:T(1,128)} %bitcast.10, bf16[2048,2048]{1,0:T(8,128)(2,1)} %weight_ref.1, f32[1,2048]{1,0:T(1,128)} %bitcast.11), custom_call_target="tpu_custom_call" | custom-call | flops 12884901888 | bytes 18874368 | tf_op jit(solution)/shard_map/table/pallas_call | solution.py:70
  30.9 0.0 all-to-all-done
  30.9 0.0 copy-start.1
  31.0 0.6 copy-done.1
  31.5 9.0 %pick.1 = bf16[8,16,128,128]{3,2,1,0:T(8,128)(2,1)} custom-call(s32[8,128]{1,0:T(8,128)} %bitcast.9, bf16[8,1024,256]{2,1,0:T(8,128)(2,1)} %table.1.table_ref), custom_call_target="tpu_custom_call" | custom-call | flops 4294967296 | bytes 8388608 | tf_op jit(solution)/shard_map/pick/pallas_call | solution.py:131
  40.6 0.0 copy-start
  40.6 10.8 %all-to-all-start.1 = ((bf16[128,128,128]{2,1,0:T(8,128)(2,1)}), bf16[128,128,128]{2,1,0:T(8,128)(2,1)}, u32[]{:S(2)}, u32[]{:S(2)}) async-start(bf16[128,128,128]{2,1,0:T(8,128)(2,1)} %bitcast.6), calls=%async_computation.1 | async-start | bytes 8388608 | tf_op jit(solution)/shard_map/all_to_all | solution.py:354
  51.4 0.0 copy-done
  51.4 0.6 broadcast_subtract_fusion
  52.0 24.6 %sort.1 = (bf16[512,4096]{1,0:T(8,128)(2,1)}, bf16[4096,256]{1,0:T(8,128)(2,1)}, bf16[4096,128]{1,0:T(8,128)(2,1)}, bf16[4096,128]{1,0:T(8,128)(2,1)}) custom-call(s32[1,4096]{1,0:T(1,128)} %bitcast.7, s32[1,4096]{1,0:T(1,128)} %bitcast.8, bf16[4096,512]{1,0:T(8,128)(2,1)} %in_ref.1), custom_call_target="tpu_custom_call" | custom-call | flops 17179869184 | bytes 16777216 | tf_op jit(solution)/shard_map/sort/pallas_call | solution.py:189
  76.6 27.4 %all-to-all-done.1 = bf16[128,128,128]{2,1,0:T(8,128)(2,1)} async-done(((bf16[128,128,128]{2,1,0:T(8,128)(2,1)}), bf16[128,128,128]{2,1,0:T(8,128)(2,1)}, u32[]{:S(2)}, u32[]{:S(2)}) %all-to-all-start.1) | async-done | bytes 4194336 | tf_op jit(solution)/shard_map/all_to_all | solution.py:354
  104.0 4.2 %entry.1 = bf16[16,16,256]{2,1,0:T(8,128)(2,1)} custom-call(bf16[512,4096]{1,0:T(8,128)(2,1)} %get-tuple-element.9.in_ref, bf16[2,16,4,128,128]{4,3,2,1,0:T(8,128)(2,1)} %bitcast.5.block_ref), custom_call_target="tpu_custom_call" | custom-call | tf_op jit(solution)/shard_map/entry/pallas_call | solution.py:235
  108.2 10.4 %all_to_all.23 = bf16[16,16,256]{2,1,0:T(8,128)(2,1)S(1)} all-to-all(bf16[16,16,256]{2,1,0:T(8,128)(2,1)} %entry.1), channel_id=1, replica_groups=mesh['task'=8,'width'=16] {'width'}, dimensions={0} | all-to-all | bytes 262144 | tf_op jit(solution)/shard_map/all_to_all | solution.py:361
  118.6 0.7 broadcast_in_dim.5
  119.3 3.8 %all-to-all-start.3 = ((bf16[16,16,256]{2,1,0:T(8,128)(2,1)}), bf16[16,16,256]{2,1,0:T(8,128)(2,1)S(1)}, u32[]{:S(2)}, u32[]{:S(2)}) async-start(bf16[16,16,256]{2,1,0:T(8,128)(2,1)} %broadcast_in_dim.5), calls=%async_computation.3 | async-start | bytes 262144 | tf_op jit(solution)/shard_map/all_to_all | solution.py:325
  123.1 2.2 %order.1.factor_ref = bf16[2048,512]{1,0:T(8,128)(2,1)S(1)} custom-call(bf16[2,16,4,128,128]{4,3,2,1,0:T(8,128)(2,1)} %bitcast.5.block_ref), custom_call_target="tpu_custom_call" | custom-call | tf_op jit(solution)/shard_map/order/pallas_call | solution.py:262
  125.3 4.0 %all-to-all-done.3.coef_ref = bf16[16,16,256]{2,1,0:T(8,128)(2,1)S(1)} async-done(((bf16[16,16,256]{2,1,0:T(8,128)(2,1)}), bf16[16,16,256]{2,1,0:T(8,128)(2,1)S(1)}, u32[]{:S(2)}, u32[]{:S(2)}) %all-to-all-start.3) | async-done | bytes 131104 | tf_op jit(solution)/shard_map/all_to_all | solution.py:325
  129.2 13.9 %exit.1 = bf16[4096,512]{1,0:T(8,128)(2,1)} custom-call(bf16[16,16,256]{2,1,0:T(8,128)(2,1)S(1)} %all-to-all-done.3.coef_ref, bf16[4096,256]{1,0:T(8,128)(2,1)} %get-tuple-element.10.low_ref, bf16[4096,128]{1,0:T(8,128)(2,1)} %get-tuple-element.11.part_ref, bf16[4096,128]{1,0:T(8,128)(2,1)} %get-tuple-element.12.name_ref, bf16[4096,512]{1,0:T(8,128)(2,1)} %base_ref.1, ...), custom_call_target="tpu_custom_call" | custom-call | tf_op jit(solution)/shard_map/exit/pallas_call | solution.py:305
  (2 shorter events, 0.0 us)
Async XLA Ops:
  1.3 29.7 %all-to-all-start = ((s32[8,1,128]{2,1,0:T(1,128)}), s32[8,1,128]{2,1,0:T(1,128)S(1)}, u32[]{:S(2)}, u32[]{:S(2)}) async-start(s32[8,1,128]{2,1,0:T(1,128)} %broadcast_in_dim.4), calls=%async_computation | async-start | bytes 8192 | tf_op jit(solution)/shard_map/all_to_all | solution.py:325
  30.9 0.6 copy-start.1
  40.6 10.8 %copy-start = (s32[4096]{0:T(1024)S(1)}, s32[4096]{0:T(1024)}, u32[]{:S(2)}) copy-start(s32[4096]{0:T(1024)} %param.15) | copy-start | bytes 49156
  40.6 63.4 %all-to-all-start.1 = ((bf16[128,128,128]{2,1,0:T(8,128)(2,1)}), bf16[128,128,128]{2,1,0:T(8,128)(2,1)}, u32[]{:S(2)}, u32[]{:S(2)}) async-start(bf16[128,128,128]{2,1,0:T(8,128)(2,1)} %bitcast.6), calls=%async_computation.1 | async-start | bytes 8388608 | tf_op jit(solution)/shard_map/all_to_all | solution.py:354
  119.3 10.0 %all-to-all-start.3 = ((bf16[16,16,256]{2,1,0:T(8,128)(2,1)}), bf16[16,16,256]{2,1,0:T(8,128)(2,1)S(1)}, u32[]{:S(2)}, u32[]{:S(2)}) async-start(bf16[16,16,256]{2,1,0:T(8,128)(2,1)} %broadcast_in_dim.5), calls=%async_computation.3 | async-start | bytes 262144 | tf_op jit(solution)/shard_map/all_to_all | solution.py:325

commit v4 on v3

--- a/solution.py
+++ b/solution.py
@@ -88,7 +88,7 @@
 
 
 def pick_kernel(id_ref, table_ref, out_ref, hot_ref, mixed_ref):
-    tasks, rows = id_ref.shape
+    tasks, _, rows = id_ref.shape
     blocks, entries, _ = table_ref.shape
     half = pl.program_id(0)
 
@@ -96,7 +96,7 @@
     def _():
         lane = iota((rows, LANES), 1).astype(F32)
         for task in range(tasks):
-            ids = jnp.broadcast_to(id_ref[task : task + 1, :].astype(F32), (LANES, rows)).T
+            ids = jnp.broadcast_to(id_ref[task, :1].astype(F32), (LANES, rows)).T
             for at in range(0, entries, LANES):
                 hot_ref[task * rows : (task + 1) * rows, at : at + LANES] = one_where(
                     ids == lane + float(at)
@@ -126,12 +126,16 @@
 
 
 def picked_rows(ids, factors):
-    tasks, rows = ids.shape
+    tasks, _, rows = ids.shape
     blocks, entries, _ = factors.shape
+    ids = pltpu.with_memory_space_constraint(ids, pltpu.MemorySpace.HBM)
     return pl.pallas_call(
         pick_kernel,
         grid=(2,),
-        in_specs=[HELD, pl.BlockSpec((blocks, entries, LANES), lambda i: (0, 0, i))],
+        in_specs=[
+            pl.BlockSpec(ids.shape, lambda i: (0, 0, 0)),
+            pl.BlockSpec((blocks, entries, LANES), lambda i: (0, 0, i)),
+        ],
         out_specs=pl.BlockSpec((tasks, 8, rows, LANES), lambda i: (0, i, 0, 0)),
         out_shape=jax.ShapeDtypeStruct((tasks, 16, rows, LANES), BF16),
         scratch_shapes=[
@@ -342,7 +346,7 @@
     width = lax.axis_size("width")
     rows_dev = task_ids.shape[0]
     me = lax.axis_index("task")
-    ids = to_all(task_ids, "task").reshape(tasks, rows_dev)
+    ids = to_all(task_ids, BOTH).reshape(tasks, width, rows_dev)
     factors = table_factors(
         embed_table,
         trunk_weight,

time: 144 us -> 146 us (1.014)
  starting transfers between devices: 23 us -> 25.6 us
    all_to_all x2, starting transfers between devices: 12.2 us -> 15.3 us  [to_all(): lax.all_to_all(jnp.broadcast_to(shard[None], (length, *shard.shape)), axi...]
  transfers between devices with their start and end apart: 3 -> 3, of which waited for: 2 -> 2; matrix products, arithmetic and copies ran while one was open for 0% -> 0% of each run, Pallas kernels for 34% -> 33%
where the time goes in v4:
time: 146 us
  Pallas kernels  75.3 us (52%)
  waiting for transfers between devices  31.4 us (22%)
  starting transfers between devices  25.6 us (18%)
  blocking collectives  10.4 us (7%)
  local copies, waits for them, and re-layouts  2.61 us (2%)
    all_to_all x1, waiting for transfers between devices, on_device(): lax.all_to_all(blocks.reshape(tasks * width, rows_dev, LANES), BOTH, 0, 0...  27.4 us
    pallas_call x1, Pallas kernels, sorted_tokens(): pl.pallas_call(sort_kernel, grid=(tokens // tile,), in_specs=[pl.BlockSpe...  24.6 us
    pallas_call x1, Pallas kernels, table_factors(): pl.pallas_call(table_kernel, grid=(early + blocks,), in_specs=[pl.BlockSp...  21.4 us
    all_to_all x2, starting transfers between devices, to_all(): lax.all_to_all(jnp.broadcast_to(shard[None], (length, *shard.shape)), axi...  15.3 us
    pallas_call x1, Pallas kernels, apply_update(): pl.pallas_call(exit_kernel, grid=(tokens // tile,), in_specs=[HELD, pl.Bl...  13.9 us
    all_to_all x1, blocking collectives, on_device(): pieces = lax.all_to_all(parts, 'width', 0, 0, tiled=True).astype(F32)  10.4 us
    all_to_all x1, starting transfers between devices, on_device(): lax.all_to_all(blocks.reshape(tasks * width, rows_dev, LANES), BOTH, 0, 0...  10.2 us
    pallas_call x1, Pallas kernels, picked_rows(): pl.pallas_call(pick_kernel, grid=(2,), in_specs=[pl.BlockSpec(ids.shape,...  9.03 us
  transfers between devices with their start and end apart: 3, of which 2 were waited for; matrix products, arithmetic and copies ran while one was open for 0% of the time, Pallas kernels for 33%

profile of v4, /device:TPU:1, one launch (start us, length us, event | category | flops | bytes accessed | tf_op | source)
XLA Modules:
  0.0 145.9 jit_solution(9096208479234091562)
XLA Ops:
  0.0 1.3 broadcast_in_dim.4
  1.3 11.5 %all-to-all-start = ((s32[128,1,128]{2,1,0:T(1,128)}), s32[128,1,128]{2,1,0:T(1,128)S(1)}, u32[]{:S(2)}, u32[]{:S(2)}) async-start(s32[128,1,128]{2,1,0:T(1,128)} %broadcast_in_dim.4), calls=%async_computation | async-start | bytes 131072 | tf_op jit(solution)/shard_map/all_to_all | solution.py:329
  12.8 21.4 %table.1.table_ref = bf16[8,1024,256]{2,1,0:T(8,128)(2,1)} custom-call(bf16[1024,1024]{1,0:T(8,128)(2,1)} %embed_ref.1, bf16[1024,2048]{1,0:T(8,128)(2,1)} %trunk_ref.1, f32[1,2048]{1,0:T(1,128)} %bitcast.10, bf16[2048,2048]{1,0:T(8,128)(2,1)} %weight_ref.1, f32[1,2048]{1,0:T(1,128)} %bitcast.11), custom_call_target="tpu_custom_call" | custom-call | flops 12884901888 | bytes 18874368 | tf_op jit(solution)/shard_map/table/pallas_call | solution.py:70
  34.2 0.0 all-to-all-done
  34.2 0.0 copy-start
  34.2 0.6 copy-done
  34.8 9.0 %pick.1 = bf16[8,16,128,128]{3,2,1,0:T(8,128)(2,1)} custom-call(s32[8,16,128]{2,1,0:T(8,128)} %bitcast.7, bf16[8,1024,256]{2,1,0:T(8,128)(2,1)} %table.1.table_ref), custom_call_target="tpu_custom_call" | custom-call | flops 4294967296 | bytes 8388608 | tf_op jit(solution)/shard_map/pick/pallas_call | solution.py:132
  43.9 0.0 copy-start.1
  43.9 10.2 %all-to-all-start.1 = ((bf16[128,128,128]{2,1,0:T(8,128)(2,1)}), bf16[128,128,128]{2,1,0:T(8,128)(2,1)}, u32[]{:S(2)}, u32[]{:S(2)}) async-start(bf16[128,128,128]{2,1,0:T(8,128)(2,1)} %bitcast.6), calls=%async_computation.1 | async-start | bytes 8388608 | tf_op jit(solution)/shard_map/all_to_all | solution.py:358
  54.1 0.0 copy-done.1
  54.1 0.6 broadcast_subtract_fusion
  54.7 24.6 %sort.1 = (bf16[512,4096]{1,0:T(8,128)(2,1)}, bf16[4096,256]{1,0:T(8,128)(2,1)}, bf16[4096,128]{1,0:T(8,128)(2,1)}, bf16[4096,128]{1,0:T(8,128)(2,1)}) custom-call(s32[1,4096]{1,0:T(1,128)} %bitcast.8, s32[1,4096]{1,0:T(1,128)} %bitcast.9, bf16[4096,512]{1,0:T(8,128)(2,1)} %in_ref.1), custom_call_target="tpu_custom_call" | custom-call | flops 17179869184 | bytes 16777216 | tf_op jit(solution)/shard_map/sort/pallas_call | solution.py:193
  79.3 27.4 %all-to-all-done.1 = bf16[128,128,128]{2,1,0:T(8,128)(2,1)} async-done(((bf16[128,128,128]{2,1,0:T(8,128)(2,1)}), bf16[128,128,128]{2,1,0:T(8,128)(2,1)}, u32[]{:S(2)}, u32[]{:S(2)}) %all-to-all-start.1) | async-done | bytes 4194336 | tf_op jit(solution)/shard_map/all_to_all | solution.py:358
  106.7 4.2 %entry.1 = bf16[16,16,256]{2,1,0:T(8,128)(2,1)} custom-call(bf16[512,4096]{1,0:T(8,128)(2,1)} %get-tuple-element.9.in_ref, bf16[2,16,4,128,128]{4,3,2,1,0:T(8,128)(2,1)} %bitcast.5.block_ref), custom_call_target="tpu_custom_call" | custom-call | tf_op jit(solution)/shard_map/entry/pallas_call | solution.py:239
  110.9 10.4 %all_to_all.21 = bf16[16,16,256]{2,1,0:T(8,128)(2,1)S(1)} all-to-all(bf16[16,16,256]{2,1,0:T(8,128)(2,1)} %entry.1), channel_id=1, replica_groups=mesh['task'=8,'width'=16] {'width'}, dimensions={0} | all-to-all | bytes 262144 | tf_op jit(solution)/shard_map/all_to_all | solution.py:365
  121.3 0.7 broadcast_in_dim.5
  122.0 3.8 %all-to-all-start.3 = ((bf16[16,16,256]{2,1,0:T(8,128)(2,1)}), bf16[16,16,256]{2,1,0:T(8,128)(2,1)S(1)}, u32[]{:S(2)}, u32[]{:S(2)}) async-start(bf16[16,16,256]{2,1,0:T(8,128)(2,1)} %broadcast_in_dim.5), calls=%async_computation.3 | async-start | bytes 262144 | tf_op jit(solution)/shard_map/all_to_all | solution.py:329
  125.8 2.2 %order.1.factor_ref = bf16[2048,512]{1,0:T(8,128)(2,1)S(1)} custom-call(bf16[2,16,4,128,128]{4,3,2,1,0:T(8,128)(2,1)} %bitcast.5.block_ref), custom_call_target="tpu_custom_call" | custom-call | tf_op jit(solution)/shard_map/order/pallas_call | solution.py:266
  128.0 4.0 %all-to-all-done.3.coef_ref = bf16[16,16,256]{2,1,0:T(8,128)(2,1)S(1)} async-done(((bf16[16,16,256]{2,1,0:T(8,128)(2,1)}), bf16[16,16,256]{2,1,0:T(8,128)(2,1)S(1)}, u32[]{:S(2)}, u32[]{:S(2)}) %all-to-all-start.3) | async-done | bytes 131104 | tf_op jit(solution)/shard_map/all_to_all | solution.py:329
  131.9 13.9 %exit.1 = bf16[4096,512]{1,0:T(8,128)(2,1)} custom-call(bf16[16,16,256]{2,1,0:T(8,128)(2,1)S(1)} %all-to-all-done.3.coef_ref, bf16[4096,256]{1,0:T(8,128)(2,1)} %get-tuple-element.10.low_ref, bf16[4096,128]{1,0:T(8,128)(2,1)} %get-tuple-element.11.part_ref, bf16[4096,128]{1,0:T(8,128)(2,1)} %get-tuple-element.12.name_ref, bf16[4096,512]{1,0:T(8,128)(2,1)} %base_ref.1, ...), custom_call_target="tpu_custom_call" | custom-call | tf_op jit(solution)/shard_map/exit/pallas_call | solution.py:309
  (2 shorter events, 0.0 us)
Async XLA Ops:
  1.3 32.9 %all-to-all-start = ((s32[128,1,128]{2,1,0:T(1,128)}), s32[128,1,128]{2,1,0:T(1,128)S(1)}, u32[]{:S(2)}, u32[]{:S(2)}) async-start(s32[128,1,128]{2,1,0:T(1,128)} %broadcast_in_dim.4), calls=%async_computation | async-start | bytes 131072 | tf_op jit(solution)/shard_map/all_to_all | solution.py:329
  34.2 0.6 copy-start
  43.9 10.2 %copy-start.1 = (s32[4096]{0:T(1024)S(1)}, s32[4096]{0:T(1024)}, u32[]{:S(2)}) copy-start(s32[4096]{0:T(1024)} %param.15) | copy-start | bytes 49156
  43.9 62.8 %all-to-all-start.1 = ((bf16[128,128,128]{2,1,0:T(8,128)(2,1)}), bf16[128,128,128]{2,1,0:T(8,128)(2,1)}, u32[]{:S(2)}, u32[]{:S(2)}) async-start(bf16[128,128,128]{2,1,0:T(8,128)(2,1)} %bitcast.6), calls=%async_computation.1 | async-start | bytes 8388608 | tf_op jit(solution)/shard_map/all_to_all | solution.py:358
  122.0 10.0 %all-to-all-start.3 = ((bf16[16,16,256]{2,1,0:T(8,128)(2,1)}), bf16[16,16,256]{2,1,0:T(8,128)(2,1)S(1)}, u32[]{:S(2)}, u32[]{:S(2)}) async-start(bf16[16,16,256]{2,1,0:T(8,128)(2,1)} %broadcast_in_dim.5), calls=%async_computation.3 | async-start | bytes 262144 | tf_op jit(solution)/shard_map/all_to_all | solution.py:329

commit v5 on v3

--- a/solution.py
+++ b/solution.py
@@ -13,6 +13,7 @@
 BOTH = ("task", "width")
 BF16 = jnp.bfloat16
 F32 = jnp.float32
+HBM = pl.BlockSpec(memory_space=pltpu.MemorySpace.HBM)
 HELD = pl.BlockSpec(memory_space=pltpu.VMEM)
 ROOM = pltpu.CompilerParams(vmem_limit_bytes=40 << 20)
 
@@ -42,7 +43,7 @@
 ):
     step = pl.program_id(0)
     hid = hidden_ref.shape[1]
-    wide = 512
+    wide = trunk_ref.shape[1]
     early = hid // wide
 
     @pl.when(step < early)
@@ -64,7 +65,7 @@
 def table_factors(embed, trunk, trunk_bias, head_weight, bias):
     entries, width = embed.shape
     hid, cols = head_weight.shape
-    early, blocks = hid // 512, cols // 256
+    early, blocks = hid // 1024, cols // 256
     first = lambda i: (0, jnp.minimum(i, early - 1))
     then = lambda i: (0, jnp.maximum(i - early, 0))
     return pl.pallas_call(
@@ -72,8 +73,8 @@
         grid=(early + blocks,),
         in_specs=[
             pl.BlockSpec(embed.shape, lambda i: (0, 0)),
-            pl.BlockSpec((width, 512), first),
-            pl.BlockSpec((1, 512), first),
+            pl.BlockSpec((width, 1024), first),
+            pl.BlockSpec((1, 1024), first),
             pl.BlockSpec((hid, 256), then),
             pl.BlockSpec((1, 256), then),
         ],
@@ -87,57 +88,77 @@
     )(embed, trunk, trunk_bias, head_weight, bias)
 
 
-def pick_kernel(id_ref, table_ref, out_ref, hot_ref, mixed_ref):
+def pick_kernel(id_ref, table_ref, out_ref, hot_ref, tile_ref, mixed_ref, sent_ref, in_sem, out_sem):
     tasks, rows = id_ref.shape
     blocks, entries, _ = table_ref.shape
-    half = pl.program_id(0)
-
-    @pl.when(half == 0)
-    def _():
-        lane = iota((rows, LANES), 1).astype(F32)
-        for task in range(tasks):
-            ids = jnp.broadcast_to(id_ref[task : task + 1, :].astype(F32), (LANES, rows)).T
-            for at in range(0, entries, LANES):
-                hot_ref[task * rows : (task + 1) * rows, at : at + LANES] = one_where(
-                    ids == lane + float(at)
-                )
-
+    loads = []
+    for half in range(2):
+        lanes = pl.ds(half * LANES, LANES)
+        loads.append(
+            pltpu.make_async_copy(
+                table_ref.at[:, :, lanes], tile_ref.at[half], in_sem.at[half]
+            )
+        )
+        loads[half].start()
+    lane = iota((rows, LANES), 1).astype(F32)
+    for task in range(tasks):
+        ids = jnp.broadcast_to(id_ref[task : task + 1, :].astype(F32), (LANES, rows)).T
+        for at in range(0, entries, LANES):
+            hot_ref[task * rows : (task + 1) * rows, at : at + LANES] = one_where(
+                ids == lane + float(at)
+            )
     group = lane_group(entries)
 
-    def mix(first):
-        for turn in (first, first + 1):
-            mixed = table_ref[0]
+    def mix(pair):
+        half, first = pair // 4, pair % 4 * 2
+        if first == 0:
+            loads[half].wait()
+        for side in range(2):
+            mixed = tile_ref[half, 0]
             for block in range(1, blocks):
-                place = jnp.asarray((block + turn) % 8, BF16)
-                mixed = jnp.where(group == place, table_ref[block], mixed)
-            mixed_ref[:, turn * LANES : (turn + 1) * LANES] = mixed
+                place = jnp.asarray((block + first + side) % 8, BF16)
+                mixed = jnp.where(group == place, tile_ref[half, block], mixed)
+            mixed_ref[pair % 2, :, side * LANES : (side + 1) * LANES] = mixed
 
     mix(0)
-    for first in range(0, 8, 2):
-        if first + 2 < 8:
-            mix(first + 2)
-        picked = product(hot_ref[...], mixed_ref[:, first * LANES : (first + 2) * LANES])
+    stores = []
+    for pair in range(8):
+        if pair + 1 < 8:
+            mix(pair + 1)
+        picked = product(hot_ref[...], mixed_ref[pair % 2])
         for side in range(2):
-            turn = first + side
+            turn = pair % 4 * 2 + side
             piece = picked[:, side * LANES : side * LANES + LANES]
             if turn:
                 piece = pltpu.roll(piece, LANES - 16 * turn, 1)
-            out_ref[:, turn] = piece.astype(BF16).reshape(tasks, rows, LANES)
-
+            sent_ref[:, 2 * pair + side] = piece.astype(BF16).reshape(tasks, rows, LANES)
+        span = pl.ds(2 * pair, 2)
+        stores.append(
+            pltpu.make_async_copy(sent_ref.at[:, span], out_ref.at[:, span], out_sem.at[pair])
+        )
+        stores[pair].start()
+    for store in stores:
+        store.wait()
 
 def picked_rows(ids, factors):
     tasks, rows = ids.shape
     blocks, entries, _ = factors.shape
+    shape = (tasks, 16, rows, LANES)
+    factors = pltpu.with_memory_space_constraint(factors, pltpu.MemorySpace.HBM)
     return pl.pallas_call(
         pick_kernel,
-        grid=(2,),
-        in_specs=[HELD, pl.BlockSpec((blocks, entries, LANES), lambda i: (0, 0, i))],
-        out_specs=pl.BlockSpec((tasks, 8, rows, LANES), lambda i: (0, i, 0, 0)),
-        out_shape=jax.ShapeDtypeStruct((tasks, 16, rows, LANES), BF16),
+        in_specs=[HELD, HBM],
+        out_specs=HBM,
+        out_shape=pltpu.MemorySpace.HBM(shape, BF16),
         scratch_shapes=[
             pltpu.VMEM((tasks * rows, entries), BF16),
-            pltpu.VMEM((entries, 8 * LANES), BF16),
-        ],
+            pltpu.VMEM((2, blocks, entries, LANES), BF16),
+            pltpu.VMEM((2, entries, 2 * LANES), BF16),
+            pltpu.VMEM(shape, BF16),
+            pltpu.SemaphoreType.DMA((2,)),
+            pltpu.SemaphoreType.DMA((8,)),
+        ],
+        compiler_params=ROOM,
         cost_estimate=cost(2 * tasks * rows * entries * 16 * LANES, 8 << 20),
         name="pick",
     )(ids, factors)

time: 144 us -> 143 us (level)
  transfers between devices with their start and end apart: 3 -> 3, of which waited for: 2 -> 2; matrix products, arithmetic and copies ran while one was open for 0% -> 0% of each run, Pallas kernels for 34% -> 33%
where the time goes in v5:
time: 143 us; the launch traced here: 142 us
  Pallas kernels  75 us (52%)
  waiting for transfers between devices  31.4 us (22%)
  starting transfers between devices  23 us (16%)
  blocking collectives  10.4 us (7%)
  local copies, waits for them, and re-layouts  1.92 us (1%)
    all_to_all x1, waiting for transfers between devices, on_device(): lax.all_to_all(blocks.reshape(tasks * width, rows_dev, LANES), BOTH, 0, 0...  27.4 us
    pallas_call x1, Pallas kernels, sorted_tokens(): pl.pallas_call(sort_kernel, grid=(tokens // tile,), in_specs=[pl.BlockSpe...  24.5 us
    pallas_call x1, Pallas kernels, table_factors(): pl.pallas_call(table_kernel, grid=(early + blocks,), in_specs=[pl.BlockSp...  20.9 us
    pallas_call x1, Pallas kernels, apply_update(): pl.pallas_call(exit_kernel, grid=(tokens // tile,), in_specs=[HELD, pl.Bl...  13.9 us
    all_to_all x2, starting transfers between devices, to_all(): lax.all_to_all(jnp.broadcast_to(shard[None], (length, *shard.shape)), axi...  12.2 us
    all_to_all x1, starting transfers between devices, on_device(): lax.all_to_all(blocks.reshape(tasks * width, rows_dev, LANES), BOTH, 0, 0...  10.8 us
    all_to_all x1, blocking collectives, on_device(): pieces = lax.all_to_all(parts, 'width', 0, 0, tiled=True).astype(F32)  10.4 us
    pallas_call x1, Pallas kernels, picked_rows(): pl.pallas_call(pick_kernel, in_specs=[HELD, HBM], out_specs=HBM, out_shap...  9.24 us
  transfers between devices with their start and end apart: 3, of which 2 were waited for; matrix products, arithmetic and copies ran while one was open for 0% of the time, Pallas kernels for 33%

profile of v5, /device:TPU:1, one launch (start us, length us, event | category | flops | bytes accessed | tf_op | source)
XLA Modules:
  0.0 142.3 jit_solution(10899008581163231449)
XLA Ops:
  0.0 1.3 broadcast_in_dim.4
  1.3 8.3 %all-to-all-start = ((s32[8,1,128]{2,1,0:T(1,128)}), s32[8,1,128]{2,1,0:T(1,128)S(1)}, u32[]{:S(2)}, u32[]{:S(2)}) async-start(s32[8,1,128]{2,1,0:T(1,128)} %broadcast_in_dim.4), calls=%async_computation | async-start | bytes 8192 | tf_op jit(solution)/shard_map/all_to_all | solution.py:346
  9.6 20.9 %table.1.table_ref = bf16[8,1024,256]{2,1,0:T(8,128)(2,1)} custom-call(bf16[1024,1024]{1,0:T(8,128)(2,1)} %embed_ref.1, bf16[1024,2048]{1,0:T(8,128)(2,1)} %trunk_ref.1, f32[1,2048]{1,0:T(1,128)} %bitcast.10, bf16[2048,2048]{1,0:T(8,128)(2,1)} %weight_ref.1, f32[1,2048]{1,0:T(1,128)} %bitcast.11), custom_call_target="tpu_custom_call" | custom-call | flops 12884901888 | bytes 18874368 | tf_op jit(solution)/shard_map/table/pallas_call | solution.py:71
  30.4 0.0 all-to-all-done
  30.4 9.2 %pick.1 = bf16[8,16,128,128]{3,2,1,0:T(8,128)(2,1)} custom-call(s32[8,128]{1,0:T(8,128)S(1)} %bitcast.6, bf16[8,1024,256]{2,1,0:T(8,128)(2,1)} %table.1.table_ref), custom_call_target="tpu_custom_call" | custom-call | flops 4294967296 | bytes 8388608 | tf_op jit(solution)/shard_map/pick/pallas_call | solution.py:148
  39.7 0.0 copy-start
  39.7 10.8 %all-to-all-start.1 = ((bf16[128,128,128]{2,1,0:T(8,128)(2,1)}), bf16[128,128,128]{2,1,0:T(8,128)(2,1)}, u32[]{:S(2)}, u32[]{:S(2)}) async-start(bf16[128,128,128]{2,1,0:T(8,128)(2,1)} %bitcast.7), calls=%async_computation.1 | async-start | bytes 8388608 | tf_op jit(solution)/shard_map/all_to_all | solution.py:375
  50.6 0.0 copy-done
  50.6 0.6 broadcast_subtract_fusion
  51.2 24.5 %sort.1 = (bf16[512,4096]{1,0:T(8,128)(2,1)}, bf16[4096,256]{1,0:T(8,128)(2,1)}, bf16[4096,128]{1,0:T(8,128)(2,1)}, bf16[4096,128]{1,0:T(8,128)(2,1)}) custom-call(s32[1,4096]{1,0:T(1,128)} %bitcast.8, s32[1,4096]{1,0:T(1,128)} %bitcast.9, bf16[4096,512]{1,0:T(8,128)(2,1)} %in_ref.1), custom_call_target="tpu_custom_call" | custom-call | flops 17179869184 | bytes 16777216 | tf_op jit(solution)/shard_map/sort/pallas_call | solution.py:210
  75.7 27.4 %all-to-all-done.1 = bf16[128,128,128]{2,1,0:T(8,128)(2,1)} async-done(((bf16[128,128,128]{2,1,0:T(8,128)(2,1)}), bf16[128,128,128]{2,1,0:T(8,128)(2,1)}, u32[]{:S(2)}, u32[]{:S(2)}) %all-to-all-start.1) | async-done | bytes 4194336 | tf_op jit(solution)/shard_map/all_to_all | solution.py:375
  103.1 4.2 %entry.1 = bf16[16,16,256]{2,1,0:T(8,128)(2,1)} custom-call(bf16[512,4096]{1,0:T(8,128)(2,1)} %get-tuple-element.9.in_ref, bf16[2,16,4,128,128]{4,3,2,1,0:T(8,128)(2,1)} %bitcast.5.block_ref), custom_call_target="tpu_custom_call" | custom-call | tf_op jit(solution)/shard_map/entry/pallas_call | solution.py:256
  107.3 10.4 %all_to_all.23 = bf16[16,16,256]{2,1,0:T(8,128)(2,1)S(1)} all-to-all(bf16[16,16,256]{2,1,0:T(8,128)(2,1)} %entry.1), channel_id=1, replica_groups=mesh['task'=8,'width'=16] {'width'}, dimensions={0} | all-to-all | bytes 262144 | tf_op jit(solution)/shard_map/all_to_all | solution.py:382
  117.7 0.7 broadcast_in_dim.5
  118.4 3.8 %all-to-all-start.3 = ((bf16[16,16,256]{2,1,0:T(8,128)(2,1)}), bf16[16,16,256]{2,1,0:T(8,128)(2,1)S(1)}, u32[]{:S(2)}, u32[]{:S(2)}) async-start(bf16[16,16,256]{2,1,0:T(8,128)(2,1)} %broadcast_in_dim.5), calls=%async_computation.3 | async-start | bytes 262144 | tf_op jit(solution)/shard_map/all_to_all | solution.py:346
  122.2 2.2 %order.1.factor_ref = bf16[2048,512]{1,0:T(8,128)(2,1)S(1)} custom-call(bf16[2,16,4,128,128]{4,3,2,1,0:T(8,128)(2,1)} %bitcast.5.block_ref), custom_call_target="tpu_custom_call" | custom-call | tf_op jit(solution)/shard_map/order/pallas_call | solution.py:283
  124.4 4.0 %all-to-all-done.3.coef_ref = bf16[16,16,256]{2,1,0:T(8,128)(2,1)S(1)} async-done(((bf16[16,16,256]{2,1,0:T(8,128)(2,1)}), bf16[16,16,256]{2,1,0:T(8,128)(2,1)S(1)}, u32[]{:S(2)}, u32[]{:S(2)}) %all-to-all-start.3) | async-done | bytes 131104 | tf_op jit(solution)/shard_map/all_to_all | solution.py:346
  128.4 13.9 %exit.1 = bf16[4096,512]{1,0:T(8,128)(2,1)} custom-call(bf16[16,16,256]{2,1,0:T(8,128)(2,1)S(1)} %all-to-all-done.3.coef_ref, bf16[4096,256]{1,0:T(8,128)(2,1)} %get-tuple-element.10.low_ref, bf16[4096,128]{1,0:T(8,128)(2,1)} %get-tuple-element.11.part_ref, bf16[4096,128]{1,0:T(8,128)(2,1)} %get-tuple-element.12.name_ref, bf16[4096,512]{1,0:T(8,128)(2,1)} %base_ref.1, ...), custom_call_target="tpu_custom_call" | custom-call | tf_op jit(solution)/shard_map/exit/pallas_call | solution.py:326
  (2 shorter events, 0.0 us)
Async XLA Ops:
  1.3 29.2 %all-to-all-start = ((s32[8,1,128]{2,1,0:T(1,128)}), s32[8,1,128]{2,1,0:T(1,128)S(1)}, u32[]{:S(2)}, u32[]{:S(2)}) async-start(s32[8,1,128]{2,1,0:T(1,128)} %broadcast_in_dim.4), calls=%async_computation | async-start | bytes 8192 | tf_op jit(solution)/shard_map/all_to_all | solution.py:346
  39.7 10.9 %copy-start = (s32[4096]{0:T(1024)S(1)}, s32[4096]{0:T(1024)}, u32[]{:S(2)}) copy-start(s32[4096]{0:T(1024)} %param.15) | copy-start | bytes 49156
  39.7 63.4 %all-to-all-start.1 = ((bf16[128,128,128]{2,1,0:T(8,128)(2,1)}), bf16[128,128,128]{2,1,0:T(8,128)(2,1)}, u32[]{:S(2)}, u32[]{:S(2)}) async-start(bf16[128,128,128]{2,1,0:T(8,128)(2,1)} %bitcast.7), calls=%async_computation.1 | async-start | bytes 8388608 | tf_op jit(solution)/shard_map/all_to_all | solution.py:375
  118.4 10.0 %all-to-all-start.3 = ((bf16[16,16,256]{2,1,0:T(8,128)(2,1)}), bf16[16,16,256]{2,1,0:T(8,128)(2,1)S(1)}, u32[]{:S(2)}, u32[]{:S(2)}) async-start(bf16[16,16,256]{2,1,0:T(8,128)(2,1)} %broadcast_in_dim.5), calls=%async_computation.3 | async-start | bytes 262144 | tf_op jit(solution)/shard_map/all_to_all | solution.py:346
